TPU v7x, 32 devices: a whole 2x2x4 slice. The times are simulated.
32 devices in a mesh: dp: 16 (over z, y, core), mp: 2 (over x).
Axes of the slice: x: 2, y: 2, z: 4, core: 2. Of those that a mesh axis runs over, the one named last changes fastest.
Arguments:
- tokens: bfloat16 [32768, 768], P(('dp', 'mp')), may hold values from -6 to 6
- lengths: int32 [64], P(('dp', 'mp')), may hold values from 32 to 512, as said below
- w_in: bfloat16 [768, 2304], P(('dp', 'mp')), may hold values from -0.21875 to 0.21875
- w_out: bfloat16 [768, 768], P(('dp', 'mp')), may hold values from -0.21875 to 0.21875
- short_conv: bfloat16 [3, 2304], P(None, ('dp', 'mp')), may hold values from -3 to 3
- cond_conv: bfloat16 [3, 768], P(None, ('dp', 'mp')), may hold values from -3 to 3
- cond_gain: bfloat16 [2, 513, 768], P(None, None, ('dp', 'mp')), may hold values from -0.29882812 to 0.29882812
- base_spectrum: bfloat16 [2, 513, 768], P(None, None, ('dp', 'mp')), may hold values from -4 to 4
- gain1: bfloat16 [768], P(('dp', 'mp')), may hold values from 0.5 to 1.5
- gain2: bfloat16 [768], P(('dp', 'mp')), may hold values from 0.5 to 1.5
- w_gate: bfloat16 [768, 3072], P('dp', 'mp'), may hold values from -0.21875 to 0.21875
- w_up: bfloat16 [768, 3072], P('dp', 'mp'), may hold values from -0.21875 to 0.21875
- w_down: bfloat16 [3072, 768], P('mp', 'dp'), may hold values from -0.109375 to 0.109375
- cotangent: bfloat16 [32768, 768], P(('dp', 'mp')), may hold values from -6 to 6
Outputs:
- mixed: bfloat16 [32768, 768], P(('dp', 'mp'))
- grad_tokens: float32 [32768, 768], P(('dp', 'mp'))
- grad_w_in: float32 [768, 2304], P(('dp', 'mp'))
- grad_w_out: float32 [768, 768], P(('dp', 'mp'))
- grad_short_conv: float32 [3, 2304], P(None, ('dp', 'mp'))
- grad_cond_conv: float32 [3, 768], P(None, ('dp', 'mp'))
- grad_cond_gain: float32 [2, 513, 768], P(None, None, ('dp', 'mp'))
- grad_base_spectrum: float32 [2, 513, 768], P(None, None, ('dp', 'mp'))
- grad_gain1: float32 [768], P(('dp', 'mp'))
- grad_gain2: float32 [768], P(('dp', 'mp'))
- grad_w_gate: float32 [768, 3072], P('dp', 'mp')
- grad_w_up: float32 [768, 3072], P('dp', 'mp')
- grad_w_down: float32 [3072, 768], P('mp', 'dp')
Inputs may be any that keep to these rules, and one draw needn't show every extreme that they name: `lengths`: each sequence's length; slots at and beyond it are padding; some sequence has 512 and some 32.
All inputs are finite; a program needn't handle non-finite values.
Results may differ from a plain program's by a relative error of at most 0.015.
Values may be sent and summed in bfloat16 or wider, within the bound.
No kernel may reach another device: no remote copies, remote signals or barrier semaphores. Data moves between devices by JAX's collectives and lax.ppermute only.
A program may use at most 320 MiB of HBM per device.

v0:
```python
import math

import jax
import jax.numpy as jnp
from jax import lax
from jax.sharding import PartitionSpec as P

EPS = 1e-05


def layer_norm(values, gain):
    centre = values - jnp.mean(values, axis=-1, keepdims=True)
    var = jnp.mean(centre * centre, axis=-1, keepdims=True)
    return centre * lax.rsqrt(var + EPS) * gain


def causal_taps(seq, taps):
    one = jnp.pad(seq, ((0, 0), (1, 0), (0, 0)))[:, :-1]
    two = jnp.pad(seq, ((0, 0), (2, 0), (0, 0)))[:, :-2]
    return taps[0] * seq + taps[1] * one + taps[2] * two


def inner_rows(left, right):
    return lax.dot_general(
        left, right, (((0,), (0,)), ((), ())), preferred_element_type=jnp.float32
    )


def times_trans(left, right):
    return lax.dot_general(
        left, right, (((1,), (1,)), ((), ())), preferred_element_type=jnp.float32
    )


def dft_tables(length):
    points = 2 * length
    freqs = jnp.arange(length + 1, dtype=jnp.int32)
    slots = jnp.arange(length, dtype=jnp.int32)
    phase = freqs[:, None] * slots[None, :] % points
    angle = phase.astype(jnp.float32) * (2.0 * math.pi / points)
    cosine = jnp.cos(angle)
    sine = jnp.sin(angle)
    forward_t = jnp.concatenate([cosine, -sine], axis=0)
    weight = jnp.where((freqs == 0) | (freqs == length), 1.0, 2.0).astype(jnp.float32) / points
    inverse_t = jnp.concatenate([(weight[:, None] * cosine).T, -(weight[:, None] * sine).T], axis=1)
    return (forward_t, inverse_t)


def long_mixer(streams, short_taps, cond_taps, cond_resp, base_resp, mask3, forward_t, inverse_t):
    seqs, length = (mask3.shape[0], mask3.shape[1])
    width = streams.shape[1] // 3
    bins = length + 1
    conv_in = causal_taps(streams.reshape(seqs, length, 3 * width), short_taps)
    gate_a = conv_in[:, :, :width]
    cond_b = conv_in[:, :, width : 2 * width]
    values = conv_in[:, :, 2 * width :] * mask3
    cond_k = causal_taps(cond_b, cond_taps) * mask3
    spectra = jnp.einsum(
        "ft,stc->sfc",
        forward_t,
        jnp.concatenate([cond_k, values], axis=-1),
        precision=lax.Precision.HIGH,
    )
    kr = spectra[:, :bins, :width]
    ki = spectra[:, bins:, :width]
    vr = spectra[:, :bins, width:]
    vi = spectra[:, bins:, width:]
    filt_r = base_resp[0] + cond_resp[0] * kr - cond_resp[1] * ki
    filt_i = base_resp[1] + cond_resp[0] * ki + cond_resp[1] * kr
    prod_r = vr * filt_r - vi * filt_i
    prod_i = vr * filt_i + vi * filt_r
    conv = jnp.einsum(
        "tf,sfc->stc",
        inverse_t,
        jnp.concatenate([prod_r, prod_i], axis=1),
        precision=lax.Precision.HIGH,
    )
    return (gate_a * conv * mask3).reshape(seqs * length, width)


def gelu_product(gate, upper):
    return jax.nn.gelu(gate, approximate=False) * upper


def shards(
    tokens,
    lengths,
    w_in,
    w_out,
    short_conv,
    cond_conv,
    cond_gain,
    base_spectrum,
    gain1,
    gain2,
    w_gate,
    w_up,
    w_down,
    cotangent,
):
    rows = tokens.shape[0]
    seqs = lengths.shape[0]
    length = rows // seqs
    full_in, full_out, short_w, cond_w, cresp_w, base_w, gain_one, gain_two = (
        lax.all_gather(w_in, ("dp", "mp"), axis=0, tiled=True),
        lax.all_gather(w_out, ("dp", "mp"), axis=0, tiled=True),
        lax.all_gather(short_conv, ("dp", "mp"), axis=1, tiled=True),
        lax.all_gather(cond_conv, ("dp", "mp"), axis=1, tiled=True),
        lax.all_gather(cond_gain, ("dp", "mp"), axis=2, tiled=True),
        lax.all_gather(base_spectrum, ("dp", "mp"), axis=2, tiled=True),
        lax.all_gather(gain1, ("dp", "mp"), axis=0, tiled=True),
        lax.all_gather(gain2, ("dp", "mp"), axis=0, tiled=True),
    )
    slots = jnp.arange(length, dtype=jnp.int32)
    mask3 = (slots[None, :] < lengths[:, None]).astype(jnp.float32)[:, :, None]
    mask = mask3.reshape(rows, 1)
    inputs = tokens.astype(jnp.float32)

    def norm_mask(values, gain):
        return layer_norm(values, gain) * mask

    norm_one, norm_one_back = jax.vjp(norm_mask, inputs, gain_one.astype(jnp.float32))
    normed = norm_one.astype(jnp.bfloat16)
    streams = jnp.dot(normed, full_in, preferred_element_type=jnp.float32)
    forward_t, inverse_t = dft_tables(length)

    def mixer_piece(zz, short_taps, cond_taps, cond_resp, base_resp):
        return long_mixer(
            zz, short_taps, cond_taps, cond_resp, base_resp, mask3, forward_t, inverse_t
        )

    gated_f, mixer_back = jax.vjp(
        mixer_piece,
        streams,
        short_w.astype(jnp.float32),
        cond_w.astype(jnp.float32),
        cresp_w.astype(jnp.float32),
        base_w.astype(jnp.float32),
    )
    gated = gated_f.astype(jnp.bfloat16)
    x_one = inputs + jnp.dot(gated, full_out, preferred_element_type=jnp.float32)
    norm_two, norm_two_back = jax.vjp(norm_mask, x_one, gain_two.astype(jnp.float32))
    normed_two = norm_two.astype(jnp.bfloat16)
    gate_w, up_w, down_w = (
        lax.all_gather(w_gate, "dp", axis=0, tiled=True),
        lax.all_gather(w_up, "dp", axis=0, tiled=True),
        lax.all_gather(w_down, "dp", axis=1, tiled=True),
    )
    gathered = lax.all_gather(normed_two, "mp", axis=0, tiled=True)
    gate_f = jnp.dot(gathered, gate_w, preferred_element_type=jnp.float32)
    up_f = jnp.dot(gathered, up_w, preferred_element_type=jnp.float32)
    act_f, act_back = jax.vjp(gelu_product, gate_f, up_f)
    act = act_f.astype(jnp.bfloat16)
    branch_out = lax.psum_scatter(
        jnp.dot(act, down_w, preferred_element_type=jnp.float32).astype(jnp.bfloat16),
        "mp",
        scatter_dimension=0,
        tiled=True,
    ).astype(jnp.float32)
    cot_all = lax.all_gather(cotangent, "mp", axis=0, tiled=True)
    d_act = times_trans(cot_all, down_w)
    grad_down = inner_rows(act, cot_all)
    d_gate_f, d_up_f = act_back(d_act)
    d_gate = d_gate_f.astype(jnp.bfloat16)
    d_up = d_up_f.astype(jnp.bfloat16)
    grad_gate = inner_rows(gathered, d_gate)
    grad_up = inner_rows(gathered, d_up)
    d_norm_two = lax.psum_scatter(
        (times_trans(d_gate, gate_w) + times_trans(d_up, up_w)).astype(jnp.bfloat16),
        "mp",
        scatter_dimension=0,
        tiled=True,
    ).astype(jnp.float32)
    group_grads = (grad_gate, grad_up, grad_down)
    grad_gate_s, grad_up_s, grad_down_s = (
        lax.psum_scatter(
            group_grads[0].astype(jnp.bfloat16), "dp", scatter_dimension=0, tiled=True
        ).astype(jnp.float32),
        lax.psum_scatter(
            group_grads[1].astype(jnp.bfloat16), "dp", scatter_dimension=0, tiled=True
        ).astype(jnp.float32),
        lax.psum_scatter(
            group_grads[2].astype(jnp.bfloat16), "dp", scatter_dimension=1, tiled=True
        ).astype(jnp.float32),
    )
    mixed = (x_one + branch_out).astype(jnp.bfloat16)
    d_x_norm_two, d_gain_two = norm_two_back(d_norm_two)
    d_x_one = cotangent.astype(jnp.float32) + d_x_norm_two
    d_branch = d_x_one.astype(jnp.bfloat16)
    grad_out = inner_rows(gated, d_branch)
    d_gated = times_trans(d_branch, full_out)
    d_streams_f, d_short, d_cond, d_cresp, d_base = mixer_back(d_gated)
    d_streams = d_streams_f.astype(jnp.bfloat16)
    grad_in = inner_rows(normed, d_streams)
    d_normed = times_trans(d_streams, full_in)
    d_x_norm_one, d_gain_one = norm_one_back(d_normed)
    grad_tokens = d_x_one + d_x_norm_one
    g_in, g_out, g_short, g_cond, g_cresp, g_base, g_gain1, g_gain2 = (
        lax.psum_scatter(grad_in, ("dp", "mp"), scatter_dimension=0, tiled=True),
        lax.psum_scatter(grad_out, ("dp", "mp"), scatter_dimension=0, tiled=True),
        lax.psum_scatter(d_short, ("dp", "mp"), scatter_dimension=1, tiled=True),
        lax.psum_scatter(d_cond, ("dp", "mp"), scatter_dimension=1, tiled=True),
        lax.psum_scatter(d_cresp, ("dp", "mp"), scatter_dimension=2, tiled=True),
        lax.psum_scatter(d_base, ("dp", "mp"), scatter_dimension=2, tiled=True),
        lax.psum_scatter(d_gain_one, ("dp", "mp"), scatter_dimension=0, tiled=True),
        lax.psum_scatter(d_gain_two, ("dp", "mp"), scatter_dimension=0, tiled=True),
    )
    return (
        mixed,
        grad_tokens,
        g_in,
        g_out,
        g_short,
        g_cond,
        g_cresp,
        g_base,
        g_gain1,
        g_gain2,
        grad_gate_s,
        grad_up_s,
        grad_down_s,
    )


def solution(mesh):
    in_specs = (
        P(("dp", "mp"), None),
        P(("dp", "mp")),
        P(("dp", "mp"), None),
        P(("dp", "mp"), None),
        P(None, ("dp", "mp")),
        P(None, ("dp", "mp")),
        P(None, None, ("dp", "mp")),
        P(None, None, ("dp", "mp")),
        P(("dp", "mp")),
        P(("dp", "mp")),
        P("dp", "mp"),
        P("dp", "mp"),
        P("mp", "dp"),
        P(("dp", "mp"), None),
    )
    out_specs = (
        P(("dp", "mp"), None),
        P(("dp", "mp"), None),
        P(("dp", "mp"), None),
        P(("dp", "mp"), None),
        P(None, ("dp", "mp")),
        P(None, ("dp", "mp")),
        P(None, None, ("dp", "mp")),
        P(None, None, ("dp", "mp")),
        P(("dp", "mp")),
        P(("dp", "mp")),
        P("dp", "mp"),
        P("dp", "mp"),
        P("mp", "dp"),
    )
    return jax.shard_map(shards, mesh=mesh, in_specs=in_specs, out_specs=out_specs, check_vma=False)
```

profile of v0, /device:TPU:0, one launch (start us, length us, event | category | flops | bytes accessed | tf_op | source)
XLA Modules:
  0.0 1208.5 jit_solution(9140501386448933691)
XLA Ops:
  18.8 42.2 %all-reduce.37 = (bf16[768]{0:T(1024)(128)(2,1)S(1)}, bf16[768]{0:T(1024)(128)(2,1)S(1)}) all-reduce(bf16[768]{0:T(1024)(128)(2,1)S(1)} %dynamic-update-slice, bf16[768]{0:T(1024)(128)(2,1)S(1)} %dynamic-update-slice.1), channel_id=1, replica_groups=mesh['dp'=16,'mp'=2] {'dp','mp'}, use_global_device_ids=true, to_apply=%add.27 | all-reduce | flops 1536 | bytes 6144
  61.1 65.9 %all-gather = bf16[32,72,3]{1,2,0:T(4,128)(2,1)S(1)} all-gather(bf16[1,72,3]{1,2,0:T(4,128)(2,1)S(1)} %bitcast.124), channel_id=1, replica_groups=mesh['dp'=16,'mp'=2] {'dp','mp'}, dimensions={0}, use_global_device_ids=true | all-gather | bytes 14256 | tf_op jit(solution)/shard_map/all_gather | solution.py:107
  127.2 63.6 %all-gather.1 = bf16[32,24,3]{1,2,0:T(4,128)(2,1)S(1)} all-gather(bf16[1,24,3]{1,2,0:T(4,128)(2,1)S(1)} %bitcast.125), channel_id=1, replica_groups=mesh['dp'=16,'mp'=2] {'dp','mp'}, dimensions={0}, use_global_device_ids=true | all-gather | bytes 4752 | tf_op jit(solution)/shard_map/all_gather | solution.py:108
  230.2 14.6 %convolution_bitcast_fusion = f32[2,1026,1536]{2,1,0:T(8,128)S(1)} fusion(f32[2,512,768]{2,1,0:T(8,128)} %get-tuple-element.126, f32[2,512,768]{2,1,0:T(8,128)} %add_multiply_fusion, f32[513,512]{1,0:T(8,128)S(1)} %copy-done.20, f32[513,512]{1,0:T(8,128)} %get-tuple-element.157), kind=kOutput, calls=%fused_computation.1 | convolution fusion | flops 9684648960 | bytes 21000192 | tf_op jit(solution)/shard_map/jvp(ft,stc->sfc)/dot_general | solution.py:58
  244.8 10.8 multiply_subtract_fusion
  261.4 11.8 fusion.43
  289.8 45.7 %all-gather.20.cloned.1.call-done = bf16[2048,768]{0,1:T(8,128)(2,1)} async-done(((bf16[1024,768]{0,1:T(8,128)(2,1)}), bf16[2048,768]{0,1:T(8,128)(2,1)}) %all-gather.20.cloned.1.call-update) | async-done | bytes 3145744 | tf_op jit(solution)/shard_map/all_gather | solution.py:149
  335.5 10.4 fusion.81
  345.8 36.2 %all-gather.28.cloned.1.call-done = bf16[2048,768]{1,0:T(8,128)(2,1)} async-done(((bf16[1024,768]{1,0:T(8,128)(2,1)}), bf16[2048,768]{1,0:T(8,128)(2,1)}) %all-gather.28.cloned.1.call-update) | async-done | bytes 3145744 | tf_op jit(solution)/shard_map/all_gather | solution.py:160
  382.0 44.5 %all-gather.26.cloned.1.call-done = bf16[1536,768]{0,1:T(8,128)(2,1)} async-done(((bf16[1536,48]{0,1:T(8,128)(2,1)}), bf16[1536,768]{0,1:T(8,128)(2,1)}) %all-gather.26.cloned.1.call-update) | async-done | bytes 2359312 | tf_op jit(solution)/shard_map/all_gather | solution.py:147
  426.5 34.1 %multiply_convert_fusion = (bf16[2048,1536]{1,0:T(8,128)(2,1)}, f32[2048,1536]{1,0:T(8,128)}, f32[2048,1536]{1,0:T(8,128)}) fusion(f32[2048,1536]{1,0:T(8,128)} %fusion.81, bf16[2048,768]{1,0:T(8,128)(2,1)} %all-gather.28.cloned.1.call-done, bf16[1536,768]{0,1:T(8,128)(2,1)} %all-gather.26.cloned.1.call-done), kind=kOutput, calls=%fused_computation.12 | convolution fusion | flops 5039456256 | bytes 49545216 | tf_op jit(solution)/shard_map/dot_general | solution.py:30
  460.6 9.2 all-gather.24.cloned.1.call-done
  469.9 21.5 %add_convert_fusion = (bf16[2048,1536]{1,0:T(8,128)(2,1)}, bf16[2048,1536]{1,0:T(8,128)(2,1)}) fusion(f32[2048,1536]{1,0:T(8,128)} %get-tuple-element.113, f32[2048,1536]{1,0:T(8,128)} %get-tuple-element.153, f32[2048,1536]{1,0:T(8,128)} %fusion.81, bf16[2048,768]{0,1:T(8,128)(2,1)S(1)} %copy-done.60, bf16[768,1536]{1,0:T(8,128)(2,1)} %all-gather.24.cloned.1.call-done), kind=kOutput, calls=%fused_computation.13 | convolution fusion | flops 4888461312 | bytes 55836672 | tf_op jit(solution)/shard_map/dot_general | solution.py:151
  491.4 7.3 fusion.82
  505.3 9.2 convolution_convert_fusion.2
  514.6 9.3 convolution_convert_fusion.1
  524.0 9.2 convolution_convert_fusion
  533.2 9.1 convolution_convert_fusion.3
  557.6 7.9 convolution_bitcast_fusion.1
  565.5 19.9 %multiply_add_fusion.6 = (f32[2,513,768]{2,1,0:T(8,128)}, f32[2,513,768]{2,1,0:T(8,128)}, f32[513,768]{1,0:T(8,128)}, f32[513,768]{1,0:T(8,128)}, f32[513,768]{1...) fusion(f32[2,513,768]{2,1,0:T(8,128)} %get-tuple-element.115, ...), kind=kLoop, calls=%fused_computation.81 | loop fusion | flops 16547328 | bytes 47278080 | tf_op jit(solution)/shard_map/transpose(jvp())/add_any | solution.py:70
  589.2 7.4 copy.101
  601.7 7.2 copy.100
  609.0 7.3 multiply_add_fusion.2
  616.3 18.2 %fusion.29 = f32[2,512,1536]{2,1,0:T(8,128)} fusion(f32[2,513,768]{2,1,0:T(8,128)} %get-tuple-element.122, f32[2,513,768]{2,1,0:T(8,128)} %get-tuple-element.121, f32[2,513,768]{2,1,0:T(8,128)} %get-tuple-element.120, f32[2,513,768]{2,1,0:T(8,128)} %get-tuple-element.119, f32[513,512]{1,0:T(8,128)} %get-tuple-element.156, f32[513,512]{1,0:T(8,128)} %get-tuple-element.157), kind=kOutput, calls=%fused_computation.61 | convolution fusion | flops 9692531712 | bytes 21000192 | tf_op jit(solution)/shard_map/transpose(jvp(ft,stc->sfc))/dot_general | solution.py:58
  634.6 9.1 multiply_reduce_fusion.10
  652.4 16.1 %multiply_reduce_fusion.2 = (f32[2304]{0:T(1024)S(1)}, f32[2304]{0:T(1024)S(1)}, f32[2304]{0:T(1024)S(1)}, f32[2,512,2304]{2,1,0:T(8,128)S(1)}, f32[2,512,2304]{2,1,0:T(8,128)S(1)}) fusion(f32[2,512,2304]{2,1,0:T(8,128)} %bitcast.101, f32[2,512,768]{2,1,0:T(8,128)} %get-tuple-element.144, f32[2,512,768]{2,1,0:T(8,128)} %fusion.35, ...), kind=kLoop, calls=%fused_computation.38 | loop fusion | flops 23586048 | bytes 47232000 | tf_op jit(solution)/shard_map/transpose(jvp())/reduce_sum | solution.py:20
  686.0 60.6 %reduce-scatter.22.cloned.1.call-done = bf16[1536,48]{0,1:T(8,128)(2,1)} async-done(((bf16[1536,768]{0,1:T(8,128)(2,1)}), bf16[1536,48]{0,1:T(8,128)(2,1)}) %reduce-scatter.22.cloned.1.call-update) | async-done | bytes 147472 | tf_op jit(solution)/shard_map/reduce_scatter | solution.py:182
  748.3 7.9 fusion.40
  757.9 40.8 %all-reduce.35 = (f32[3,2304]{1,0:T(4,128)S(1)}, f32[3,768]{1,0:T(4,128)S(1)}, f32[768]{0:T(1024)S(1)}, f32[768]{0:T(1024)S(1)}) all-reduce(f32[3,2304]{1,0:T(4,128)S(1)} %pad_add_fusion.3, f32[3,768]{1,0:T(4,128)S(1)} %pad_add_fusion.4, f32[768]{0:T(1024)S(1)} %get-tuple-element.92, ...), channel_id=6, replica_groups=mesh['dp'=16,'mp'=2] {'dp','mp'}, use_global_device_ids=true, to_apply=%region_15.16.clone | all-reduce | flops 10752 | bytes 86016
  813.1 158.6 %all-reduce.40.cloned.1.call-done = (f32[2,513,768]{1,0,2:T(2,128)}, f32[2,513,768]{1,0,2:T(2,128)}) async-done(((f32[2,513,768]{1,0,2:T(2,128)}, f32[2,513,768]{1,0,2:T(2,128)}), (f32[2,513,768]{1,0,2:T(2,128)}, f32[2,513,768]{1,0,2:T(2,128)})) %all-reduce.40.cloned.1.call-update) | async-done | bytes 6303760
  974.9 102.5 %reduce-scatter.16.cloned.1.call-done = f32[24,768]{1,0:T(8,128)} async-done(((f32[768,768]{1,0:T(8,128)}), f32[24,768]{1,0:T(8,128)}) %reduce-scatter.16.cloned.1.call-update) | async-done | bytes 73744 | tf_op jit(solution)/shard_map/reduce_scatter | solution.py:200
  1077.4 124.3 %reduce-scatter.14.cloned.1.call-done = f32[24,2304]{1,0:T(8,128)} async-done(((f32[768,2304]{1,0:T(8,128)}), f32[24,2304]{1,0:T(8,128)}) %reduce-scatter.14.cloned.1.call-update) | async-done | bytes 221200 | tf_op jit(solution)/shard_map/reduce_scatter | solution.py:199
  (264 shorter events, 150.7 us)
Async XLA Ops:
  7.2 189.2 %all-gather.16.cloned.1.call-start = ((), (), s32[]{:S(2)}) async-start(), calls=%async_computation.9 | async-start | bytes 2027520 | tf_op jit(solution)/shard_map/all_gather | solution.py:109
  7.9 197.9 %all-gather.14.cloned.1.call-start = ((), (), s32[]{:S(2)}) async-start(), calls=%async_computation.8 | async-start | bytes 2027520 | tf_op jit(solution)/shard_map/all_gather | solution.py:110
  8.7 206.6 %all-gather.12.cloned.1.call-start = ((), (), s32[]{:S(2)}) async-start(), calls=%async_computation.7 | async-start | bytes 3649536 | tf_op jit(solution)/shard_map/all_gather | solution.py:105
  9.4 263.8 %all-gather.18.cloned.1.call-start = ((), (), s32[]{:S(2)}) async-start(), calls=%async_computation.10 | async-start | bytes 1216512 | tf_op jit(solution)/shard_map/all_gather | solution.py:106
  10.0 279.8 %all-gather.22.cloned.1.call-start = ((), (), s32[]{:S(2)}) async-start(), calls=%async_computation.12 | async-start | bytes 2506752 | tf_op jit(solution)/shard_map/all_gather | solution.py:145
  10.6 324.9 %all-gather.20.cloned.1.call-start = ((), (), s32[]{:S(2)}) async-start(), calls=%async_computation.11 | async-start | bytes 4718592 | tf_op jit(solution)/shard_map/all_gather | solution.py:149
  15.7 45.4 %copy-start.56 = (bf16[3,72]{1,0:T(4,128)(2,1)S(1)}, bf16[3,72]{1,0:T(4,128)(2,1)}, u32[]{:S(2)}) copy-start(bf16[3,72]{1,0:T(4,128)(2,1)} %param.18) | copy-start | bytes 1300
  15.7 111.5 %copy-start.57 = (bf16[3,24]{1,0:T(4,128)(2,1)S(1)}, bf16[3,24]{1,0:T(4,128)(2,1)}, u32[]{:S(2)}) copy-start(bf16[3,24]{1,0:T(4,128)(2,1)} %param.19) | copy-start | bytes 436
  17.5 255.8 %copy-start.5 = (bf16[1024,768]{0,1:T(8,128)(2,1)}, bf16[1024,768]{0,1:T(8,128)(2,1)S(1)}, u32[]{:S(2)}) copy-start(bf16[1024,768]{0,1:T(8,128)(2,1)S(1)} %copy.87) | copy-start | bytes 4718596
  17.7 197.5 %copy-start.40 = (f32[1024]{0:T(1024)}, f32[1024]{0:T(1024)S(1)}, u32[]{:S(2)}) copy-start(f32[1024]{0:T(1024)S(1)} %broadcast_multiply_fusion.5) | copy-start | bytes 12292
  18.2 180.0 %copy-start.48 = (f32[1024]{0:T(1024)}, f32[1024]{0:T(1024)S(1)}, u32[]{:S(2)}) copy-start(f32[1024]{0:T(1024)S(1)} %fusion.39) | copy-start | bytes 12292
  18.2 197.0 %copy-start.52 = (f32[1024]{0:T(1024)}, f32[1024]{0:T(1024)S(1)}, u32[]{:S(2)}) copy-start(f32[1024]{0:T(1024)S(1)} %fusion.69) | copy-start | bytes 12292
  18.3 243.0 %copy-start.24 = (f32[2,512]{1,0:T(2,128)}, f32[2,512]{1,0:T(2,128)S(1)}, u32[]{:S(2)}) copy-start(f32[2,512]{1,0:T(2,128)S(1)} %get-tuple-element.147) | copy-start | bytes 12292
  18.3 259.5 %copy-start.28 = (f32[1,4,2,128]{3,1,2,0:T(4,128)}, f32[1,4,2,128]{3,1,2,0:T(4,128)S(1)}, u32[]{:S(2)}) copy-start(f32[1,4,2,128]{3,1,2,0:T(4,128)S(1)} %copy.114) | copy-start | bytes 12292
  61.1 154.2 %copy-start.54 = (f32[768]{0:T(1024)}, f32[768]{0:T(1024)S(1)}, u32[]{:S(2)}) copy-start(f32[768]{0:T(1024)S(1)} %convert_element_type.124) | copy-start | bytes 9220
  127.2 94.2 %copy-start.32 = (f32[2304]{0:T(1024)}, f32[2304]{0:T(1024)S(1)}, u32[]{:S(2)}) copy-start(f32[2304]{0:T(1024)S(1)} %get-tuple-element.96) | copy-start | bytes 27652
  127.2 94.2 %copy-start.34 = (f32[2304]{0:T(1024)}, f32[2304]{0:T(1024)S(1)}, u32[]{:S(2)}) copy-start(f32[2304]{0:T(1024)S(1)} %get-tuple-element.97) | copy-start | bytes 27652
  127.2 94.2 %copy-start.36 = (f32[2304]{0:T(1024)}, f32[2304]{0:T(1024)S(1)}, u32[]{:S(2)}) copy-start(f32[2304]{0:T(1024)S(1)} %get-tuple-element.98) | copy-start | bytes 27652
  196.4 81.4 %copy-start.30 = (f32[768]{0:T(1024)}, f32[768]{0:T(1024)S(1)}, u32[]{:S(2)}) copy-start(f32[768]{0:T(1024)S(1)} %convert_element_type.136) | copy-start | bytes 9220
  225.0 36.4 %copy-start.3 = (f32[2,512,2304]{2,1,0:T(8,128)}, f32[2,512,2304]{2,1,0:T(8,128)S(1)}, u32[]{:S(2)}) copy-start(f32[2,512,2304]{2,1,0:T(8,128)S(1)} %multiply_add_fusion) | copy-start | bytes 28311556
  280.4 101.6 %all-gather.28.cloned.1.call-start = ((), (), s32[]{:S(2)}) async-start(), calls=%async_computation.16 | async-start | bytes 4718592 | tf_op jit(solution)/shard_map/all_gather | solution.py:160
  281.2 145.4 %all-gather.26.cloned.1.call-start = ((), (), s32[]{:S(2)}) async-start(), calls=%async_computation.14 | async-start | bytes 2506752 | tf_op jit(solution)/shard_map/all_gather | solution.py:147
  281.9 187.9 %all-gather.24.cloned.1.call-start = ((), (), s32[]{:S(2)}) async-start(), calls=%async_computation.13 | async-start | bytes 2506752 | tf_op jit(solution)/shard_map/all_gather | solution.py:146
  282.7 264.8 %reduce-scatter.12.cloned.1.call-start = ((), (), s32[]{:S(2)}) async-start(), calls=%async_computation.17 | async-start | bytes 4718592 | tf_op jit(solution)/shard_map/reduce_scatter | solution.py:168
  345.8 124.0 %copy-start.60 = (bf16[2048,768]{0,1:T(8,128)(2,1)S(1)}, bf16[2048,768]{0,1:T(8,128)(2,1)}, u32[]{:S(2)}) copy-start(bf16[2048,768]{0,1:T(8,128)(2,1)} %all-gather.20.cloned.1.call-done) | copy-start | bytes 9437188
  505.2 177.5 %reduce-scatter.18.cloned.1.call-start = ((), (), s32[]{:S(2)}) async-start(), calls=%async_computation.20 | async-start | bytes 2506752 | tf_op jit(solution)/shard_map/reduce_scatter | solution.py:176
  514.6 169.8 %reduce-scatter.20.cloned.1.call-start = ((), (), s32[]{:S(2)}) async-start(), calls=%async_computation.21 | async-start | bytes 2506752 | tf_op jit(solution)/shard_map/reduce_scatter | solution.py:179
  523.9 222.7 %reduce-scatter.22.cloned.1.call-start = ((), (), s32[]{:S(2)}) async-start(), calls=%async_computation.22 | async-start | bytes 2506752 | tf_op jit(solution)/shard_map/reduce_scatter | solution.py:182
  533.2 266.7 %reduce-scatter.10.cloned.1.call-start = ((), (), s32[]{:S(2)}) async-start(), calls=%async_computation.15 | async-start | bytes 4718592 | tf_op jit(solution)/shard_map/reduce_scatter | solution.py:154
  542.4 429.4 %all-reduce.40.cloned.1.call-start = ((), (), s32[]{:S(2)}) async-start(), calls=%async_computation.23 | async-start | bytes 15728640
  608.9 468.5 %reduce-scatter.16.cloned.1.call-start = ((), (), s32[]{:S(2)}) async-start(), calls=%async_computation.19 | async-start | bytes 2433024 | tf_op jit(solution)/shard_map/reduce_scatter | solution.py:200
  652.3 549.4 %reduce-scatter.14.cloned.1.call-start = ((), (), s32[]{:S(2)}) async-start(), calls=%async_computation.18 | async-start | bytes 7299072 | tf_op jit(solution)/shard_map/reduce_scatter | solution.py:199
  (55 other events, 432.6 us)
Sparse Core Ops, SparseCore 0:
  10.9 59.3 all-gather.15
  73.2 55.3 all-gather.13
  131.5 59.2 all-gather.11
  193.5 52.8 all-gather.17
  248.6 41.1 all-gather.21
  291.7 43.6 all-gather.19
  337.0 44.9 all-gather.27
  384.3 42.2 all-gather.25
  428.8 40.9 all-gather.23
  505.4 42.1 reduce-scatter.11
  551.7 62.9 reduce-scatter.17
  618.4 61.9 reduce-scatter.19
  684.6 61.9 reduce-scatter.21
  748.7 43.1 reduce-scatter.9
  798.7 172.9 all-reduce.39
  978.3 99.0 reduce-scatter.15
  1083.5 118.1 reduce-scatter.13
where the time goes:
time: 1210 us
  waiting for transfers between devices  596 us (49%)
  blocking collectives  213 us (18%)
  matrix products  197 us (16%)
  other arithmetic  132 us (11%)
  local copies, waits for them, and re-layouts  55.5 us (5%)
  between operations  15.1 us (1%)
    unnamed x18, waiting for transfers between devices  164 us
    reduce_scatter x1, waiting for transfers between devices, shards(): lax.psum_scatter(grad_in, ('dp', 'mp'), scatter_dimension=0, tiled=True)  124 us
    reduce_scatter x1, waiting for transfers between devices, shards(): lax.psum_scatter(grad_out, ('dp', 'mp'), scatter_dimension=0, tiled=True)  102 us
    unnamed x2, blocking collectives  83.1 us
    all_gather x1, blocking collectives, shards(): lax.all_gather(short_conv, ('dp', 'mp'), axis=1, tiled=True)  65.9 us
    all_gather x1, blocking collectives, shards(): lax.all_gather(cond_conv, ('dp', 'mp'), axis=1, tiled=True)  63.6 us
    reduce_scatter x1, waiting for transfers between devices, shards(): lax.psum_scatter(group_grads[2].astype(jnp.bfloat16), 'dp', scatter_dimen...  60.6 us
    dot_general x5, matrix products, times_trans(): lax.dot_general(left, right, (((1,), (1,)), ((), ())), preferred_element_...  57.2 us
  transfers between devices with their start and end apart: 17, of which 10 were waited for; matrix products, arithmetic and copies ran while one was open for 28% of the time, Pallas kernels for 0%

commit v1 on v0

v1 whole, which is shorter than its diff:
```python
import functools
import math

import jax
import jax.numpy as jnp
import numpy as np
from jax import lax
from jax.experimental import pallas as pl
from jax.experimental.pallas import tpu as pltpu
from jax.sharding import PartitionSpec as P

EPS = 1e-05
AXES = ("dp", "mp")
F32 = jnp.float32
BF16 = jnp.bfloat16
NN = (((1,), (0,)), ((), ()))
NT = (((1,), (1,)), ((), ()))
TN = (((0,), (0,)), ((), ()))
RSQRT2 = np.float32(math.sqrt(0.5))
RSQRT2PI = np.float32(1.0 / math.sqrt(2.0 * math.pi))
CB = 256
RB = 256
VMEM = pl.BlockSpec(memory_space=pltpu.VMEM)
SMEM = pl.BlockSpec(memory_space=pltpu.SMEM)
ANY = pl.BlockSpec(memory_space=pl.ANY)


def dot(left, right, dims=NN):
    return lax.dot_general(left, right, dims, preferred_element_type=F32)


def sds(shape, dtype):
    return jax.ShapeDtypeStruct(shape, dtype)


def params(name=None):
    return pltpu.CompilerParams(vmem_limit_bytes=58 * 2**20)


def cost(flops, nbytes):
    return pl.CostEstimate(flops=int(flops), bytes_accessed=int(nbytes), transcendentals=0)


class Plan:
    def __init__(self, ndp, nmp):
        self.ndp, self.nmp, self.n = ndp, nmp, ndp * nmp
        self.core = nmp
        self.y = [0, nmp * 2] if ndp >= 4 else [0]
        self.z = [nmp * 4 * k for k in range(ndp // 4)]
        self.x = list(range(nmp))

    def send(self, array, mask):
        return lax.ppermute(array, AXES, [(i, i ^ mask) for i in range(self.n)])

    def gather(self, own, route):
        cur, order = own[None], [0]
        for group in route:
            parts = [cur] + [self.send(cur, m) for m in group[1:]]
            cur = jnp.concatenate(parts, axis=0) if len(parts) > 1 else cur
            order = [o ^ m for m in group for o in order]
        return cur, self.send(cur, self.core), order

    def gather_rows(self, own, route, mp_index):
        cur, order = own[None], [0]
        for group in route:
            parts = [cur] + [self.send(cur, m) for m in group[1:]]
            if group is self.x:
                step = 1
                while step < self.nmp:
                    odd = (mp_index & step) != 0
                    parts = [jnp.where(odd, parts[k ^ step], parts[k]) for k in range(self.nmp)]
                    step *= 2
                cur = jnp.concatenate(parts, axis=1)
            else:
                cur = jnp.concatenate(parts, axis=0)
                order = [o ^ m for m in group for o in order]
        return cur, self.send(cur, self.core), [o // self.nmp for o in order]

    def route_order(self, route, with_x):
        order = [0]
        for group in route:
            if group is self.x and not with_x:
                continue
            order = [o ^ m for o in order for m in group]
        return order if with_x else [o // self.nmp for o in order]

    def scatter(self, keep, far, route):
        total = keep.astype(F32) + self.send(far, self.core).astype(F32)
        for group in route:
            total = total.reshape((len(group), -1) + total.shape[1:])
            got = [self.send(total[k].astype(BF16), m) for k, m in enumerate(group) if m]
            total = sum([g.astype(F32) for g in got], total[0])
        return total.reshape(total.shape[1:])

    def scatter_rows(self, keep, far, route, mp_index):
        total = keep.astype(F32) + self.send(far, self.core).astype(F32)
        for group in route:
            if group is self.x:
                rows = total.shape[1] // self.nmp
                part = lambda m: lax.dynamic_slice_in_dim(total, (mp_index ^ m) * rows, rows, axis=1)
                got = [self.send(part(m).astype(BF16), m) for m in group[1:]]
                total = sum([g.astype(F32) for g in got], part(0))
            else:
                total = total.reshape((len(group), -1) + total.shape[1:])
                got = [self.send(total[k].astype(BF16), m) for k, m in enumerate(group) if m]
                total = sum([g.astype(F32) for g in got], total[0])
        return total.reshape(total.shape[1:])


def shift_down(value, count, row):
    return jnp.where(row >= count, pltpu.roll(value, count, 0), 0.0)


def shift_up(value, count, row):
    length = value.shape[0]
    return jnp.where(row < length - count, pltpu.roll(value, length - count, 0), 0.0)


def taps(value, w, row):
    return w[0:1] * value + w[1:2] * shift_down(value, 1, row) + w[2:3] * shift_down(value, 2, row)


def taps_back(grad, w, row):
    one, two = shift_up(grad, 1, row), shift_up(grad, 2, row)
    return w[0:1] * grad + w[1:2] * one + w[2:3] * two, one, two


def tap_sums(grads, value):
    return jnp.concatenate([jnp.sum(g * value, axis=0, keepdims=True) for g in grads], axis=0)


def normalise(value):
    centre = value - jnp.mean(value, axis=-1, keepdims=True)
    scale = lax.rsqrt(jnp.mean(centre * centre, axis=-1, keepdims=True) + EPS)
    return centre * scale, scale


def normalise_back(grad, unit, scale, gain):
    dx = grad * gain
    first = jnp.mean(dx, axis=-1, keepdims=True)
    second = jnp.mean(dx * unit, axis=-1, keepdims=True)
    return scale * (dx - first - unit * second)


def row_mask(lens, start, rows, length):
    seq = start // length
    base = start - seq * length
    return ((lax.broadcasted_iota(jnp.int32, (rows, 1), 0) + base) < lens[seq]).astype(F32)


def cmul(pr, pi, qr, qi, slot0):
    cross = pi * qi
    return pr * qr - jnp.where(slot0, 0.0, cross), jnp.where(slot0, cross, pr * qi + pi * qr)


def cmul_conj(pr, pi, qr, qi, slot0):
    cross = pi * qi
    return pr * qr + jnp.where(slot0, 0.0, cross), jnp.where(slot0, cross, pi * qr - pr * qi)


def load_rows(dst, near, far, order, dp_ref, rows, sems):
    if order is None:
        return [pltpu.make_async_copy(near, dst, sems.at[0])]
    out = []
    for s, rel in enumerate(order):
        for k, src in enumerate((near, far)):
            at = pl.multiple_of((dp_ref[0] ^ (rel ^ k)) * rows, rows)
            out.append(pltpu.make_async_copy(src.at[s], dst.at[pl.ds(at, rows)], sems.at[2 * s + k]))
    return out


def store_rows(src, near, far, order, dp_ref, rows, cols, sems):
    out = []
    for s, rel in enumerate(order):
        for k, dst in enumerate((near, far)):
            at = pl.multiple_of((dp_ref[0] ^ (rel ^ k)) * rows, rows)
            out.append(pltpu.make_async_copy(src.at[pl.ds(at, rows), cols], dst.at[s], sems.at[2 * s + k]))
    return out


def mixer_in_kernel(order, rows, length, dp, lens, x, gain, short, cond, tab, near, far, n1, z, kk, vv, w_full, w, sems, wsem):
    copies = load_rows(w, near, far, order, dp, rows, sems)
    for c in copies:
        c.start()
    tokens, width = x.shape
    keep = pltpu.make_async_copy(w.at[:, pl.ds(0, 3 * width)], w_full, wsem)

    @pl.loop(0, tokens // RB)
    def _(m):
        start = pl.multiple_of(m * RB, RB)
        unit, _ = normalise(x[pl.ds(start, RB), :].astype(F32))
        n1[pl.ds(start, RB), :] = (unit * gain[...] * row_mask(lens, start, RB, length)).astype(BF16)

    for c in copies:
        c.wait()
    keep.start()
    row = lax.broadcasted_iota(jnp.int32, (length, 1), 0)
    blocks = width // CB

    @pl.loop(0, blocks * (tokens // length))
    def _(step):
        seq, cb = step // blocks, lax.rem(step, blocks)
        rs = pl.ds(pl.multiple_of(seq * length, length), length)
        mask = (row < lens[seq]).astype(F32)
        zs = []
        for stream in (1, 2, 0):
            cs = pl.ds(pl.multiple_of(stream * width + cb * CB, CB), CB)
            val = dot(n1[rs, :], w[:, cs])
            z[rs, cs] = val.astype(BF16)
            if stream:
                zs.append(taps(val, short[:, cs], row))
        cs = pl.ds(pl.multiple_of(cb * CB, CB), CB)
        k = taps(zs[0], cond[:, cs], row) * mask
        kk[seq, :, cs] = dot(tab[...], k.astype(BF16)).astype(BF16)
        vv[seq, :, cs] = dot(tab[...], (zs[1] * mask).astype(BF16)).astype(BF16)

    keep.wait()


def filtered(half, spec, kr, ki, slot0):
    br, bi, gr, gi = (spec[n * half : (n + 1) * half, :] for n in range(4))
    tr, ti = cmul(gr, gi, kr, ki, slot0)
    return br + tr, bi + ti, gr, gi


def mixer_out_kernel(order, rows, length, dp, lens, x, gain, short, tabt, kk, vv, z, near, far, o, conv, x1, n2, spec_t, w_out, g2, sems):
    copies = load_rows(g2, near, far, order, dp, rows, sems)
    for c in copies:
        c.start()
    tokens, width = x.shape
    half = length
    for c in copies:
        c.wait()
    row = lax.broadcasted_iota(jnp.int32, (length, 1), 0)
    slot0 = row == 0
    scale = jnp.where(slot0, 1.0, 2.0) * np.float32(0.5 / length)
    w_out[...] = g2[:, :width]

    @pl.loop(0, width // CB)
    def _(cb):
        cs = pl.ds(pl.multiple_of(cb * CB, CB), CB)
        spec = jnp.transpose(g2[cs, width:].astype(F32), (1, 0))
        spec_t[:, cs] = spec.astype(BF16)
        for seq in range(tokens // length):
            rs = slice(seq * length, (seq + 1) * length)
            kr, ki = kk[seq, :half, cs].astype(F32), kk[seq, half:, cs].astype(F32)
            vr, vi = vv[seq, :half, cs].astype(F32), vv[seq, half:, cs].astype(F32)
            hr, hi, _, _ = filtered(half, spec, kr, ki, slot0)
            yr, yi = cmul(vr, vi, hr, hi, slot0)
            y = jnp.concatenate([(yr * scale).astype(BF16), (yi * scale).astype(BF16)], axis=0)
            out = dot(tabt[...], y)
            conv[rs, cs] = out.astype(BF16)
            a = taps(z[rs, cs].astype(F32), short[:, cs], row)
            o[rs, cs] = (a * out * (row < lens[seq]).astype(F32)).astype(BF16)

    @pl.loop(0, tokens // RB)
    def _(m):
        start = pl.multiple_of(m * RB, RB)
        rs = pl.ds(start, RB)
        val = x[rs, :].astype(F32) + dot(o[rs, :], w_out[...])
        x1[rs, :] = val
        unit, _ = normalise(val)
        n2[rs, :] = (unit * gain[...] * row_mask(lens, start, RB, length)).astype(BF16)


def ffn_kernel(orders, rows, first, dp, n2, c, *refs):
    parts = len(orders)
    refs = list(refs)
    acc_in, dn_in = (None, None) if first else (refs.pop(0), refs.pop(0))
    gathered = [(refs.pop(0), refs.pop(0)) for _ in range(parts)]
    acc, dn = refs.pop(0), refs.pop(0)
    outs = [(refs.pop(0), refs.pop(0)) for _ in range(parts)]
    w, g, act, dg, du, sem_in, sem_out = refs
    tokens = n2.shape[0]
    hidden = w.shape[3]
    loads, stores = [], []
    for p, (gather_order, scatter_order) in enumerate(orders):
        cols = gathered[p][0].shape[3]
        nmp = hidden // cols
        ins, out = [], []
        for s, rel in enumerate(gather_order):
            for k, src in enumerate(gathered[p]):
                at = pl.multiple_of((dp[0] ^ ((rel // nmp) ^ k)) * rows, rows)
                ins.append(pltpu.make_async_copy(src.at[s], w.at[p, :, pl.ds(at, rows), pl.ds((rel % nmp) * cols, cols)], sem_in.at[p, 2 * s + k]))
        for s, rel in enumerate(scatter_order):
            for k, dst in enumerate(outs[p]):
                at = pl.multiple_of((dp[0] ^ ((rel // nmp) ^ k)) * rows, rows)
                out.append(pltpu.make_async_copy(g.at[p, :, pl.ds(at, rows), pl.ds((rel % nmp) * cols, cols)], dst.at[s], sem_out.at[p, 2 * s + k]))
        loads.append(ins)
        stores.append(out)
    for ins in loads:
        for copy in ins:
            copy.start()
    for p in range(parts):
        for copy in loads[p]:
            copy.wait()

        @pl.loop(0, hidden // 256)
        def _(h):
            hs = pl.ds(pl.multiple_of(h * 256, 256), 256)

            @pl.loop(0, tokens // 512)
            def _(m):
                ms = pl.ds(pl.multiple_of(m * 512, 512), 512)
                gate = dot(n2[ms, :], w[p, 0, :, hs])
                up = dot(n2[ms, :], w[p, 1, :, hs])
                dact = dot(c[ms, :], w[p, 2, :, hs])
                cdf = 0.5 + 0.5 * lax.erf(gate * RSQRT2)
                soft = gate * cdf
                slope = cdf + gate * (jnp.exp(-0.5 * gate * gate) * RSQRT2PI)
                act[ms, hs] = (soft * up).astype(BF16)
                dg[ms, hs] = (dact * up * slope).astype(BF16)
                du[ms, hs] = (dact * soft).astype(BF16)

        @pl.loop(0, hidden // 256)
        def _(h):
            hs = pl.ds(pl.multiple_of(h * 256, 256), 256)
            g[p, 0, :, hs] = dot(n2[...], dg[:, hs], TN).astype(BF16)
            g[p, 1, :, hs] = dot(n2[...], du[:, hs], TN).astype(BF16)
            g[p, 2, :, hs] = dot(c[...], act[:, hs], TN).astype(BF16)

        for copy in stores[p]:
            copy.start()

        @pl.loop(0, tokens // RB)
        def _(m):
            ms = pl.ds(pl.multiple_of(m * RB, RB), RB)
            out = dot(act[ms, :], w[p, 2], NT)
            back = dot(dg[ms, :], w[p, 0], NT) + dot(du[ms, :], w[p, 1], NT)
            if p == 0 and first:
                acc[ms, :] = out
                dn[ms, :] = back
            elif p == 0:
                acc[ms, :] = acc_in[ms, :] + out
                dn[ms, :] = dn_in[ms, :] + back
            else:
                acc[ms, :] += out
                dn[ms, :] += back

    for out in stores:
        for copy in out:
            copy.wait()


def spectrum_back_kernel(order, rows, length, dp, lens, x1, acc, dn, c, gain, o, w_out, spec_t, kk, vv, z, conv, short, tab,
                         mixed, dx1, d_gain, dk, dv, da, near, far, dm1, g2, sems):
    tokens, width = x1.shape
    half = length
    d_gain[...] = jnp.zeros_like(d_gain)

    @pl.loop(0, tokens // RB)
    def _(m):
        start = pl.multiple_of(m * RB, RB)
        rs = pl.ds(start, RB)
        mixed[rs, :] = (x1[rs, :] + acc[rs, :]).astype(BF16)
        unit, scale = normalise(x1[rs, :])
        grad = dn[rs, :] * row_mask(lens, start, RB, length)
        d_gain[...] += jnp.sum(grad * unit, axis=0, keepdims=True)
        val = c[rs, :].astype(F32) + normalise_back(grad, unit, scale, gain[...])
        dx1[rs, :] = val
        dm1[rs, :] = val.astype(BF16)

    @pl.loop(0, width // CB)
    def _(cb):
        cs = pl.ds(pl.multiple_of(cb * CB, CB), CB)
        g2[:, cs] = dot(o[...], dm1[:, cs], TN).astype(BF16)

    row = lax.broadcasted_iota(jnp.int32, (length, 1), 0)
    slot0 = row == 0
    scale = jnp.where(slot0, 1.0, 2.0) * np.float32(0.5 / length)

    @pl.loop(0, width // CB)
    def _(cb):
        cs = pl.ds(pl.multiple_of(cb * CB, CB), CB)
        spec = spec_t[:, cs].astype(F32)
        sums = [0.0] * 4
        for seq in range(tokens // length):
            rs = slice(seq * length, (seq + 1) * length)
            d_o = dot(dm1[rs, :], w_out[cs, :], NT) * (row < lens[seq]).astype(F32)
            da[rs, cs] = (d_o * conv[rs, cs].astype(F32)).astype(BF16)
            a = taps(z[rs, cs].astype(F32), short[:, cs], row)
            dy = dot(tab[...], (d_o * a).astype(BF16))
            dyr, dyi = dy[:half] * scale, dy[half:] * scale
            kr, ki = kk[seq, :half, cs].astype(F32), kk[seq, half:, cs].astype(F32)
            vr, vi = vv[seq, :half, cs].astype(F32), vv[seq, half:, cs].astype(F32)
            hr, hi, gr, gi = filtered(half, spec, kr, ki, slot0)
            dvr, dvi = cmul_conj(dyr, dyi, hr, hi, slot0)
            dv[seq, :half, cs], dv[seq, half:, cs] = dvr.astype(BF16), dvi.astype(BF16)
            dhr, dhi = cmul_conj(dyr, dyi, vr, vi, slot0)
            dkr, dki = cmul_conj(dhr, dhi, gr, gi, slot0)
            dk[seq, :half, cs], dk[seq, half:, cs] = dkr.astype(BF16), dki.astype(BF16)
            ggr, ggi = cmul_conj(dhr, dhi, kr, ki, slot0)
            sums = [s + t for s, t in zip(sums, (dhr, dhi, ggr, ggi))]
        for n, val in enumerate(sums):
            g2[cs, width + n * half : width + (n + 1) * half] = jnp.transpose(val, (1, 0)).astype(BF16)

    copies = store_rows(g2, near, far, order, dp, rows, slice(None), sems)
    for copy in copies:
        copy.start()
    for copy in copies:
        copy.wait()


def mixer_back_kernel(orders, rows, length, dp, lens, n1, z, dk, dv, da, short, cond, tabt, *refs):
    parts = len(orders)
    dz, d_short, d_cond = refs[:3]
    outs = [refs[3 + 2 * p : 5 + 2 * p] for p in range(parts)]
    g, sems = refs[3 + 2 * parts :]
    tokens, width = n1.shape
    row = lax.broadcasted_iota(jnp.int32, (length, 1), 0)
    d_short[...] = jnp.zeros_like(d_short)
    d_cond[...] = jnp.zeros_like(d_cond)

    @pl.loop(0, width // CB)
    def _(cb):
        for seq in range(tokens // length):
            rs = slice(seq * length, (seq + 1) * length)
            cols = [pl.ds(pl.multiple_of(n * width + cb * CB, CB), CB) for n in range(3)]
            cs = cols[0]
            mask = (row < lens[seq]).astype(F32)
            dvm = dot(tabt[...], dv[seq, :, cs]) * mask
            dkm = dot(tabt[...], dk[seq, :, cs]) * mask
            zb = z[rs, cols[1]].astype(F32)
            b = taps(zb, short[:, cols[1]], row)
            db, one, two = taps_back(dkm, cond[:, cs], row)
            d_cond[:, cs] += tap_sums((dkm, one, two), b)
            for n, grad in enumerate((da[rs, cs].astype(F32), db, dvm)):
                val, one, two = taps_back(grad, short[:, cols[n]], row)
                zn = zb if n == 1 else z[rs, cols[n]].astype(F32)
                d_short[:, cols[n]] += tap_sums((grad, one, two), zn)
                dz[rs, cols[n]] = val.astype(BF16)

    @pl.loop(0, 3 * width // CB)
    def _(cb):
        cs = pl.ds(pl.multiple_of(cb * CB, CB), CB)
        g[:, cs] = dot(n1[...], dz[:, cs], TN).astype(BF16)

    copies, at = [], 0
    for p in range(parts):
        cols = outs[p][0].shape[2]
        copies += store_rows(g, *outs[p], orders[p], dp, rows, pl.ds(at, cols), sems.at[p])
        at += cols
    for copy in copies:
        copy.start()
    for copy in copies:
        copy.wait()


def token_back_kernel(length, lens, x, dz, w, dx1, gain, grad, d_gain):
    tokens, width = x.shape
    d_gain[...] = jnp.zeros_like(d_gain)

    @pl.loop(0, tokens // RB)
    def _(m):
        start = pl.multiple_of(m * RB, RB)
        rs = pl.ds(start, RB)
        d_n1 = dot(dz[rs, :], w[...], NT) * row_mask(lens, start, RB, length)
        unit, scale = normalise(x[rs, :].astype(F32))
        d_gain[...] += jnp.sum(d_n1 * unit, axis=0, keepdims=True)
        grad[rs, :] = dx1[rs, :] + normalise_back(d_n1, unit, scale, gain[...])


def dft_table(length):
    phase = np.outer(np.arange(length), np.arange(length)) % (2 * length)
    angle = phase * (math.pi / length)
    real, imag = np.cos(angle), -np.sin(angle)
    imag[0] = np.cos(math.pi * np.arange(length))
    return np.concatenate([real, imag], axis=0).astype(np.float32).astype(jnp.bfloat16)


def pack_spectrum(spec, half):
    return jnp.concatenate([spec[0, :half], spec[0, half:], spec[1, 1:half]], axis=0).T


def unpack_spectrum(flat, half):
    real, imag = flat[:, :half].T, flat[:, half:].T
    zero = jnp.zeros_like(real[:1])
    return jnp.stack([jnp.concatenate([real, imag[:1]], axis=0), jnp.concatenate([zero, imag[1:], zero], axis=0)])


def shards(ndp, nmp, tokens, lengths, w_in, w_out, short_conv, cond_conv, cond_gain, base_spectrum, gain1, gain2, w_gate, w_up, w_down, cotangent):
    plan = Plan(ndp, nmp)
    rows_all, width = tokens.shape
    seqs = lengths.shape[0]
    length = rows_all // seqs
    half = length
    dp_index, mp_index = lax.axis_index("dp"), lax.axis_index("mp")
    dp = dp_index.reshape(1).astype(jnp.int32)
    routes = ((plan.z, plan.y, plan.x), (plan.z, plan.x, plan.y))
    back_routes = ((plan.y, plan.x, plan.z), (plan.x, plan.y, plan.z))

    small = jnp.concatenate([short_conv.reshape(-1), cond_conv.reshape(-1), gain1, gain2])
    chan = w_in.shape[0]
    slots = small.shape[0] // chan
    small = jnp.pad(small.reshape(chan, slots), ((0, 0), (0, 128 - slots)))
    own1 = jnp.concatenate([w_in, small], axis=1)
    own2 = jnp.concatenate([w_out, pack_spectrum(base_spectrum, half), pack_spectrum(cond_gain, half)], axis=1)
    ffn = jnp.stack([w_gate, w_up, w_down.T])
    rows = width // ndp
    group = ffn.shape[2]
    split = 384 if group % 1536 == 0 else 128
    pieces = [ffn[:, :, k : k + split] for k in range(0, group, split)]

    near1, far1, order1 = plan.gather_rows(own1, routes[0], mp_index)
    near2, far2, order2 = plan.gather_rows(own2, routes[1], mp_index)
    gathered = [plan.gather(piece, routes[k % 2]) for k, piece in enumerate(pieces)]

    full = jnp.concatenate([near1[:, :, 3 * width :], far1[:, :, 3 * width :]], axis=0).astype(F32)
    rel = jnp.array(order1 + [r ^ 1 for r in order1], jnp.int32)
    hot = (rel[None, :] == (jnp.arange(ndp, dtype=jnp.int32) ^ dp_index)[:, None]).astype(F32)
    full = jnp.dot(hot, full[:, :, :slots].reshape(ndp, -1), precision=lax.Precision.HIGHEST)
    full = full.reshape(ndp * nmp, chan * slots)
    cuts = np.cumsum([short_conv.size, cond_conv.size, chan])
    short = full[:, : cuts[0]].reshape(-1, 3, 3 * chan).transpose(1, 0, 2).reshape(3, 3 * width)
    cond = full[:, cuts[0] : cuts[1]].reshape(-1, 3, chan).transpose(1, 0, 2).reshape(3, width)
    gain_one = full[:, cuts[1] : cuts[2]].reshape(1, width)
    gain_two = full[:, cuts[2] :].reshape(1, width)

    if rows % 16:

        def whole(near, far, order):
            both = jnp.concatenate([near, far], axis=0)
            index = jnp.array(order + [r ^ 1 for r in order], jnp.int32)
            place = jnp.argsort(index ^ dp_index)
            return jnp.take(both, place, axis=0).reshape(width, -1)

        near1 = whole(near1, far1, order1)
        near2 = whole(near2, far2, order2)
        order1 = order2 = None

    tab = jnp.asarray(dft_table(length))
    tabt = jnp.asarray(dft_table(length).T)
    sems = pltpu.SemaphoreType.DMA((ndp,))
    spectra = sds((seqs, 2 * half, width), BF16)

    n1, z, kk, vv, w_full = pl.pallas_call(
        functools.partial(mixer_in_kernel, order1, rows, length),
        out_shape=[sds((rows_all, width), BF16), sds((rows_all, 3 * width), BF16), spectra, spectra, sds((width, 3 * width), BF16)],
        in_specs=[SMEM, SMEM, VMEM, VMEM, VMEM, VMEM, VMEM, ANY, ANY],
        out_specs=[VMEM, VMEM, VMEM, VMEM, ANY],
        scratch_shapes=[pltpu.VMEM((width, 3 * width + 128), BF16), sems, pltpu.SemaphoreType.DMA],
        compiler_params=params(),
        cost_estimate=cost(2 * rows_all * width * (3 * width + 4 * half), 30e6),
        name="mixer_in",
    )(dp, lengths, tokens, gain_one, short, cond, tab, near1, far1)

    cols2 = width + 4 * half
    o, conv, x1, n2, spec_t, w_out_full = pl.pallas_call(
        functools.partial(mixer_out_kernel, order2, rows, length),
        out_shape=[sds((rows_all, width), BF16), sds((rows_all, width), BF16), sds((rows_all, width), F32), sds((rows_all, width), BF16),
                   sds((4 * half, width), BF16), sds((width, width), BF16)],
        in_specs=[SMEM, SMEM, VMEM, VMEM, VMEM, VMEM, VMEM, VMEM, VMEM, ANY, ANY],
        out_specs=[VMEM] * 6,
        scratch_shapes=[pltpu.VMEM((width, cols2), BF16), sems],
        compiler_params=params(),
        cost_estimate=cost(2 * rows_all * width * (width + 2 * half), 30e6),
        name="mixer_out",
    )(dp, lengths, tokens, gain_two, short, tabt, kk, vv, z, near2, far2)

    calls = [[k, k + 1] if k + 1 < len(pieces) else [k] for k in range(0, len(pieces), 2)]
    state = []
    ffn_grads = [None] * len(pieces)
    hidden = split * nmp
    for call in calls:
        orders = [(gathered[k][2], plan.route_order(back_routes[k % 2], True)) for k in call]
        blocks = [a for k in call for a in gathered[k][:2]]
        count = len(call)
        got = pl.pallas_call(
            functools.partial(ffn_kernel, orders, rows, not state),
            out_shape=[sds((rows_all, width), F32)] * 2 + [sds(a.shape, BF16) for a in blocks],
            in_specs=[SMEM, VMEM, VMEM] + [VMEM] * len(state) + [ANY] * (2 * count),
            out_specs=[VMEM, VMEM] + [ANY] * (2 * count),
            scratch_shapes=[pltpu.VMEM((count, 3, width, hidden), BF16)] * 2 + [pltpu.VMEM((rows_all, hidden), BF16)] * 3
            + [pltpu.SemaphoreType.DMA((count, ndp * nmp))] * 2,
            compiler_params=params(),
            cost_estimate=cost(18 * rows_all * width * hidden * count, 30e6),
            name="ffn",
        )(dp, n2, cotangent, *state, *blocks)
        state = got[:2]
        for j, k in enumerate(call):
            ffn_grads[k] = got[2 + 2 * j : 4 + 2 * j]
    acc, dn = state
    sums = [plan.scatter(near, far, back_routes[k % 2]) for k, (near, far) in enumerate(ffn_grads)]
    grad_ffn = jnp.concatenate(sums, axis=2)

    g2_order = plan.route_order(back_routes[1], False)
    cube = sds((ndp // 2, rows, cols2), BF16)
    mixed, dx1, d_gain2, dk, dv, da, near, far = pl.pallas_call(
        functools.partial(spectrum_back_kernel, g2_order, rows, length),
        out_shape=[sds((rows_all, width), BF16), sds((rows_all, width), F32), sds((1, width), F32), spectra, spectra,
                   sds((rows_all, width), BF16), cube, cube],
        in_specs=[SMEM, SMEM] + [VMEM] * 14,
        out_specs=[VMEM] * 6 + [ANY] * 2,
        scratch_shapes=[pltpu.VMEM((rows_all, width), BF16), pltpu.VMEM((width, cols2), BF16), sems],
        compiler_params=params(),
        cost_estimate=cost(2 * rows_all * width * (2 * width + 2 * half), 40e6),
        name="spectrum_back",
    )(dp, lengths, x1, acc, dn, cotangent, gain_two, o, w_out_full, spec_t, kk, vv, z, conv, short, tab)
    grad2 = plan.scatter_rows(near, far, back_routes[1], mp_index)

    cols = (3 * width) // 2
    orders = [plan.route_order(route, False) for route in back_routes]
    cube = sds((ndp // 2, rows, cols), BF16)
    dz, d_short, d_cond, *blocks = pl.pallas_call(
        functools.partial(mixer_back_kernel, orders, rows, length),
        out_shape=[sds((rows_all, 3 * width), BF16), sds((3, 3 * width), F32), sds((3, width), F32)] + [cube] * 4,
        in_specs=[SMEM, SMEM] + [VMEM] * 8,
        out_specs=[VMEM] * 3 + [ANY] * 4,
        scratch_shapes=[pltpu.VMEM((width, 3 * width), BF16), pltpu.SemaphoreType.DMA((2, ndp))],
        compiler_params=params(),
        cost_estimate=cost(2 * rows_all * width * (3 * width + 4 * half), 30e6),
        name="mixer_back",
    )(dp, lengths, n1, z, dk, dv, da, short, cond, tabt)
    grad_in = jnp.concatenate(
        [plan.scatter_rows(blocks[2 * p], blocks[2 * p + 1], back_routes[p], mp_index) for p in range(2)], axis=1
    )

    grad_tokens, d_gain1 = pl.pallas_call(
        functools.partial(token_back_kernel, length),
        out_shape=[sds((rows_all, width), F32), sds((1, width), F32)],
        in_specs=[SMEM] + [VMEM] * 5,
        out_specs=[VMEM] * 2,
        compiler_params=params(),
        cost_estimate=cost(2 * rows_all * width * 3 * width, 20e6),
        name="token_back",
    )(lengths, tokens, dz, w_full, dx1, gain_one)

    flat = jnp.concatenate(
        [
            d_short.reshape(3, ndp * nmp, 3 * chan).transpose(1, 0, 2).reshape(ndp * nmp, -1),
            d_cond.reshape(3, ndp * nmp, chan).transpose(1, 0, 2).reshape(ndp * nmp, -1),
            d_gain1.reshape(-1, chan),
            d_gain2.reshape(-1, chan),
        ],
        axis=1,
    )
    me = dp_index * nmp + mp_index
    order = plan.route_order(back_routes[0], True)
    order = jnp.array(order + [r ^ plan.core for r in order], jnp.int32)
    hot = ((order ^ me)[:, None] == jnp.arange(ndp * nmp, dtype=jnp.int32)[None, :]).astype(F32)
    flat = jnp.dot(hot, flat, precision=lax.Precision.HIGHEST)
    count = ndp * nmp // 2
    total = flat[:count] + plan.send(flat[count:], plan.core)
    for grp in back_routes[0]:
        total = total.reshape((len(grp), -1) + total.shape[1:])
        total = sum([plan.send(total[k], m) for k, m in enumerate(grp) if m], total[0])
    total = total.reshape(-1)
    cuts = np.cumsum([short_conv.size, cond_conv.size, chan])

    return (
        mixed,
        grad_tokens,
        grad_in,
        grad2[:, :width],
        total[: cuts[0]].reshape(short_conv.shape),
        total[cuts[0] : cuts[1]].reshape(cond_conv.shape),
        unpack_spectrum(grad2[:, width + 2 * half :], half),
        unpack_spectrum(grad2[:, width : width + 2 * half], half),
        total[cuts[1] : cuts[2]],
        total[cuts[2] :],
        grad_ffn[0],
        grad_ffn[1],
        grad_ffn[2].T,
    )


def solution(mesh):
    rows = P(AXES, None)
    cols = P(None, AXES)
    deep = P(None, None, AXES)
    flat = P(AXES)
    in_specs = (rows, flat, rows, rows, cols, cols, deep, deep, flat, flat, P("dp", "mp"), P("dp", "mp"), P("mp", "dp"), rows)
    out_specs = (rows, rows, rows, rows, cols, cols, deep, deep, flat, flat, P("dp", "mp"), P("dp", "mp"), P("mp", "dp"))
    body = functools.partial(shards, mesh.shape["dp"], mesh.shape["mp"])
    return jax.shard_map(body, mesh=mesh, in_specs=in_specs, out_specs=out_specs, check_vma=False)
```

time: 1210 us -> 549 us (0.45)
  waiting for transfers between devices: 596 us -> 201 us
  blocking collectives: 213 us -> 0 us
  matrix products: 197 us -> 0.42 us
  Pallas kernels: 0 us -> 183 us
  other arithmetic: 132 us -> 15.4 us
  starting transfers between devices: 0.68 us -> 111 us
  local copies, waits for them, and re-layouts: 55.5 us -> 30.4 us
  between operations: 15.1 us -> 1.87 us
    reduce_scatter x7 -> x0, waiting for transfers between devices: 289 us -> none  [the longest x1 124 us: shards(): lax.psum_scatter(grad_in, ('dp', 'mp'), scatter_dimension=0, tiled=True)]
    ppermute x0 -> x84, waiting for transfers between devices: none -> 201 us  [send(): return lax.ppermute(array, AXES, [(i, i ^ mask) for i in range(self.n)])]
    dot_general x19 -> x2, matrix products: 197 us -> 0.42 us  [the longest x1 0.23 us: shards(): flat = jnp.dot(hot, flat, precision=lax.Precision.HIGHEST)]
    pallas_call x0 -> x7, Pallas kernels: none -> 183 us  [the longest x2 72.6 us: shards(): pl.pallas_call(functools.partial(ffn_kernel, orders, rows, not state), ou...]
    unnamed x18 -> x0, waiting for transfers between devices: 164 us -> none
    all_gather x9 -> x0, waiting for transfers between devices: 143 us -> none  [the longest x1 45.7 us: shards(): gathered = lax.all_gather(normed_two, 'mp', axis=0, tiled=True)]
    all_gather x2 -> x0, blocking collectives: 130 us -> none  [the longest x1 65.9 us: shards(): lax.all_gather(short_conv, ('dp', 'mp'), axis=1, tiled=True)]
    ppermute x0 -> x84, starting transfers between devices: none -> 111 us  [send(): return lax.ppermute(array, AXES, [(i, i ^ mask) for i in range(self.n)])]
  transfers between devices with their start and end apart: 17 -> 84, of which waited for: 10 -> 38; matrix products, arithmetic and copies ran while one was open for 28% -> 7% of each run, Pallas kernels for 0% -> 14%
where the time goes in v1:
time: 549 us; the launch traced here: 543 us
  waiting for transfers between devices  201 us (37%)
  Pallas kernels  183 us (33%)
  starting transfers between devices  111 us (20%)
  local copies, waits for them, and re-layouts  30.4 us (6%)
  other arithmetic  15.4 us (3%)
    ppermute x84, waiting for transfers between devices, send(): return lax.ppermute(array, AXES, [(i, i ^ mask) for i in range(self.n)])  201 us
    ppermute x84, starting transfers between devices, send(): return lax.ppermute(array, AXES, [(i, i ^ mask) for i in range(self.n)])  111 us
    pallas_call x2, Pallas kernels, shards(): pl.pallas_call(functools.partial(ffn_kernel, orders, rows, not state), ou...  72.6 us
    pallas_call x1, Pallas kernels, shards(): pl.pallas_call(functools.partial(spectrum_back_kernel, g2_order, rows, le...  31.6 us
    pallas_call x1, Pallas kernels, shards(): pl.pallas_call(functools.partial(mixer_back_kernel, orders, rows, length)...  27.8 us
    pallas_call x1, Pallas kernels, shards(): pl.pallas_call(functools.partial(mixer_out_kernel, order2, rows, length),...  19.8 us
    pallas_call x1, Pallas kernels, shards(): pl.pallas_call(functools.partial(mixer_in_kernel, order1, rows, length),...  19.5 us
    pallas_call x1, Pallas kernels, shards(): pl.pallas_call(functools.partial(token_back_kernel, length), out_shape=[s...  12 us
  transfers between devices with their start and end apart: 84, of which 38 were waited for; matrix products, arithmetic and copies ran while one was open for 7% of the time, Pallas kernels for 14%

profile of v1, /device:TPU:0, one launch (start us, length us, event | category | flops | bytes accessed | tf_op | source)
XLA Modules:
  0.0 543.3 jit_solution(16242010002580983352)
XLA Ops:
  2.0 3.1 collective-permute-start.18
  8.5 3.5 collective-permute-start.13
  17.1 8.1 %collective-permute-start.1 = (bf16[1,24,2432]{2,1,0:T(8,128)(2,1)S(1)}, bf16[1,24,2432]{2,1,0:T(8,128)(2,1)S(1)}, u32[]{:S(2)}, u32[]{:S(2)}) collective-permute-start(bf16[1,24,2432]{2,1,0:T(8,128)(2,1)S(1)} %fusion.17), channel_id=1, source_target_pairs={{0,16},{1,17},{2,18},{3,19},{4,20},{5,21},{6,22},{7,23},{8,24},{9,... | collective-permute-start | bytes 350216 | tf_op jit(solution)/shard_map/ppermute | solution.py:53
  29.4 5.7 %collective-permute-start.31 = (bf16[1,3,48,384]{3,2,1,0:T(8,128)(2,1)S(1)}, bf16[1,3,48,384]{3,2,1,0:T(8,128)(2,1)S(1)}, u32[]{:S(2)}, u32[]{:S(2)}) collective-permute-start(bf16[1,3,48,384]{3,2,1,0:T(8,128)(2,1)S(1)} %get-tuple-element.139), channel_id=1, source_target_pairs={{0,16},{1,17},{2,18},{3,19},{4,20},{5,21},{6,22},{7,23},{8,24},{9,... | collective-permute-start | bytes 331784 | tf_op jit(solution)/shard_map/ppermute | solution.py:53
  39.6 5.9 %collective-permute-done.31 = bf16[1,3,48,384]{3,2,1,0:T(8,128)(2,1)S(1)} collective-permute-done((bf16[1,3,48,384]{3,2,1,0:T(8,128)(2,1)S(1)}, bf16[1,3,48,384]{3,2,1,0:T(8,128)(2,1)S(1)}, u32[]{:S(2)}, u32[]{:S(2)}) %collective-permute-start.31) | collective-permute-done | bytes 110624 | tf_op jit(solution)/shard_map/ppermute | solution.py:53
  76.4 9.1 %collective-permute-done.3 = bf16[4,24,2432]{2,1,0:T(8,128)(2,1)S(1)} collective-permute-done((bf16[4,24,2432]{2,1,0:T(8,128)(2,1)S(1)}, bf16[4,24,2432]{2,1,0:T(8,128)(2,1)S(1)}, u32[]{:S(2)}, u32[]{:S(2)}) %collective-permute-start.3) | collective-permute-done | bytes 466976 | tf_op jit(solution)/shard_map/ppermute | solution.py:53
  87.1 4.7 collective-permute-done.9
  94.0 16.9 %collective-permute-done.4 = bf16[8,24,2432]{2,1,0:T(8,128)(2,1)S(1)} collective-permute-done((bf16[8,24,2432]{2,1,0:T(8,128)(2,1)S(1)}, bf16[8,24,2432]{2,1,0:T(8,128)(2,1)S(1)}, u32[]{:S(2)}, u32[]{:S(2)}) %collective-permute-start.4) | collective-permute-done | bytes 933920 | tf_op jit(solution)/shard_map/ppermute | solution.py:53
  118.1 19.6 %collective-permute-done.10 = bf16[4,48,2816]{2,1,0:T(8,128)(2,1)S(1)} collective-permute-done((bf16[4,48,2816]{2,1,0:T(8,128)(2,1)S(1)}, bf16[4,48,2816]{2,1,0:T(8,128)(2,1)S(1)}, u32[]{:S(2)}, u32[]{:S(2)}) %collective-permute-start.10) | collective-permute-done | bytes 1081376 | tf_op jit(solution)/shard_map/ppermute | solution.py:53
  141.9 9.6 %collective-permute-done.34 = bf16[8,3,48,384]{3,2,1,0:T(8,128)(2,1)S(1)} collective-permute-done((bf16[8,3,48,384]{3,2,1,0:T(8,128)(2,1)S(1)}, bf16[8,3,48,384]{3,2,1,0:T(8,128)(2,1)S(1)}, u32[]{:S(2)}, u32[]{:S(2)}) %collective-permute-start.34) | collective-permute-done | bytes 884768 | tf_op jit(solution)/shard_map/ppermute | solution.py:53
  161.2 19.5 %mixer_in.1 = (bf16[1024,768]{1,0:T(8,128)(2,1)}, bf16[1024,2304]{1,0:T(8,128)(2,1)}, bf16[2,1024,768]{2,1,0:T(8,128)(2,1)}, bf16[2,1024,768]{2,1,0:T(8,128)(2,1)}, bf16[768,2304]{1,0:T(8,128)(2,1)}) custom-call(s32[1]{0:T(128)} %bitcast.dp, s32[2]{0:T(128)} %lens.9, bf16[1024,768]{1,0:T(8,128)(2,1)} %x.7, f32[1,768]{1,0:T(1,128)} %reshape.308.gain, ...), custom_call_target="tpu_custom_call" | custom-call | flops 6845104128 | bytes 30000000 | tf_op jit(solution)/shard_map/mixer_in/pallas_call | solution.py:536
  180.7 19.8 %mixer_out.1 = (bf16[1024,768]{1,0:T(8,128)(2,1)}, bf16[1024,768]{1,0:T(8,128)(2,1)}, f32[1024,768]{1,0:T(8,128)}, bf16[1024,768]{1,0:T(8,128)(2,1)}, bf16[2048,...) custom-call(s32[1]{0:T(128)} %bitcast.dp, s32[2]{0:T(128)} %lens.9, bf16[1024,768]{1,0:T(8,128)(2,1)} %x.7, ...), custom_call_target="tpu_custom_call" | custom-call | flops 2818572288 | bytes 30000000 | tf_op jit(solution)/shard_map/mixer_out/pallas_call | solution.py:548
  200.5 35.1 %ffn.2 = (f32[1024,768]{1,0:T(8,128)}, f32[1024,768]{1,0:T(8,128)}, bf16[16,3,48,384]{3,2,1,0:T(8,128)(2,1)}, bf16[16,3,48,384]{3,2,1,0:T(8,128)(2,1)}, bf16[16,...) custom-call(s32[1]{0:T(128)} %bitcast.dp, bf16[1024,768]{1,0:T(8,128)(2,1)} %get-tuple-element.57.n2, ...), custom_call_target="tpu_custom_call" | custom-call | flops 21743271936 | bytes 30000000 | tf_op jit(solution)/shard_map/ffn/pallas_call | solution.py:568
  235.7 37.5 %ffn.3 = (f32[1024,768]{1,0:T(8,128)}, f32[1024,768]{1,0:T(8,128)}, bf16[16,3,48,384]{3,2,1,0:T(8,128)(2,1)}, bf16[16,3,48,384]{3,2,1,0:T(8,128)(2,1)}, bf16[16,...) custom-call(s32[1]{0:T(128)} %bitcast.dp, bf16[1024,768]{1,0:T(8,128)(2,1)} %get-tuple-element.57.n2, ...), custom_call_target="tpu_custom_call" | custom-call | flops 21743271936 | bytes 30000000 | tf_op jit(solution)/shard_map/ffn/pallas_call | solution.py:568
  273.2 31.6 %spectrum_back.1 = (bf16[1024,768]{1,0:T(8,128)(2,1)}, f32[1024,768]{1,0:T(8,128)}, f32[1,768]{1,0:T(1,128)}, bf16[2,1024,768]{2,1,0:T(8,128)(2,1)}, bf16[2,1024...) custom-call(s32[1]{0:T(128)} %bitcast.dp, s32[2]{0:T(128)} %lens.9, ...), custom_call_target="tpu_custom_call" | custom-call | flops 4026531840 | bytes 40000000 | tf_op jit(solution)/shard_map/spectrum_back/pallas_call | solution.py:588
  304.8 27.8 %mixer_back.1 = (bf16[1024,2304]{1,0:T(8,128)(2,1)}, f32[3,2304]{1,0:T(4,128)}, f32[3,768]{1,0:T(4,128)}, bf16[8,48,1152]{2,1,0:T(8,128)(2,1)}, bf16[8,48,1152]{...) custom-call(s32[1]{0:T(128)} %bitcast.dp, s32[2]{0:T(128)} %lens.9, ...), custom_call_target="tpu_custom_call" | custom-call | flops 6845104128 | bytes 30000000 | tf_op jit(solution)/shard_map/mixer_back/pallas_call | solution.py:604
  332.7 12.0 %token_back.1 = (f32[1024,768]{1,0:T(8,128)}, f32[1,768]{1,0:T(1,128)}) custom-call(s32[2]{0:T(128)} %lens.9, bf16[1024,768]{1,0:T(8,128)(2,1)} %x.7, bf16[1024,2304]{1,0:T(8,128)(2,1)} %get-tuple-element.71.dz, bf16[768,2304]{1,0:T(8,128)(2,1)} %get-tuple-element.72.w, f32[1024,768]{1,0:T(8,128)} %get-tuple-element.73.dx1, f32[1,768]{1,0:T(1,128)} %reshape.308.gain), custom_call_target="tpu_custom_call" | custom-call | flops 3623878656 | bytes 20000000 | tf_op jit(solution)/shard_map/token_back/pallas_call | solution.py:618
  348.4 3.1 collective-permute-done.55
  360.7 3.1 collective-permute-done.59
  369.2 5.8 %collective-permute-done.37 = bf16[4,48,1152]{2,1,0:T(8,128)(2,1)S(1)} collective-permute-done((bf16[4,48,1152]{2,1,0:T(8,128)(2,1)S(1)}, bf16[4,48,1152]{2,1,0:T(8,128)(2,1)S(1)}, u32[]{:S(2)}, u32[]{:S(2)}) %collective-permute-start.37) | collective-permute-done | bytes 442400 | tf_op jit(solution)/shard_map/ppermute | solution.py:53
  376.6 4.1 collective-permute-done.43
  381.5 3.1 collective-permute-done.38
  386.1 3.0 collective-permute-start.40
  415.2 13.6 %collective-permute-done.61 = bf16[8,3,48,384]{3,2,1,0:T(8,128)(2,1)S(1)} collective-permute-done((bf16[8,3,48,384]{3,2,1,0:T(8,128)(2,1)S(1)}, bf16[8,3,48,384]{3,2,1,0:T(8,128)(2,1)S(1)}, u32[]{:S(2)}, u32[]{:S(2)}) %collective-permute-start.61) | collective-permute-done | bytes 884768 | tf_op jit(solution)/shard_map/ppermute | solution.py:53
  431.7 16.1 %collective-permute-done.73 = bf16[8,3,48,384]{3,2,1,0:T(8,128)(2,1)S(1)} collective-permute-done((bf16[8,3,48,384]{3,2,1,0:T(8,128)(2,1)S(1)}, bf16[8,3,48,384]{3,2,1,0:T(8,128)(2,1)S(1)}, u32[]{:S(2)}, u32[]{:S(2)}) %collective-permute-start.73) | collective-permute-done | bytes 884768 | tf_op jit(solution)/shard_map/ppermute | solution.py:53
  450.7 31.6 %collective-permute-done.62 = bf16[4,3,48,384]{3,2,1,0:T(8,128)(2,1)S(1)} collective-permute-done((bf16[4,3,48,384]{3,2,1,0:T(8,128)(2,1)S(1)}, bf16[4,3,48,384]{3,2,1,0:T(8,128)(2,1)S(1)}, u32[]{:S(2)}, u32[]{:S(2)}) %collective-permute-start.62) | collective-permute-done | bytes 442400 | tf_op jit(solution)/shard_map/ppermute | solution.py:53
  485.6 5.8 %collective-permute-done.74 = bf16[4,3,48,384]{3,2,1,0:T(8,128)(2,1)S(1)} collective-permute-done((bf16[4,3,48,384]{3,2,1,0:T(8,128)(2,1)S(1)}, bf16[4,3,48,384]{3,2,1,0:T(8,128)(2,1)S(1)}, u32[]{:S(2)}, u32[]{:S(2)}) %collective-permute-start.74) | collective-permute-done | bytes 442400 | tf_op jit(solution)/shard_map/ppermute | solution.py:53
  503.4 3.4 collective-permute-done.70
  507.4 6.7 %collective-permute-start.81 = (bf16[1,3,48,384]{3,2,1,0:T(8,128)(2,1)S(1)}, bf16[1,3,48,384]{3,2,1,0:T(8,128)(2,1)S(1)}, u32[]{:S(2)}, u32[]{:S(2)}) collective-permute-start(bf16[1,3,48,384]{3,2,1,0:T(8,128)(2,1)S(1)} %get-tuple-element.126), channel_id=1, source_target_pairs={{0,8},{1,9},{2,10},{3,11},{4,12},{5,13},{6,14},{7,15},{8,0},{9,1},... | collective-permute-start | bytes 331784 | tf_op jit(solution)/shard_map/ppermute | solution.py:53
  519.0 6.4 %collective-permute-done.82 = bf16[1,3,48,384]{3,2,1,0:T(8,128)(2,1)S(1)} collective-permute-done((bf16[1,3,48,384]{3,2,1,0:T(8,128)(2,1)S(1)}, bf16[1,3,48,384]{3,2,1,0:T(8,128)(2,1)S(1)}, u32[]{:S(2)}, u32[]{:S(2)}) %collective-permute-start.82) | collective-permute-done | bytes 110624 | tf_op jit(solution)/shard_map/ppermute | solution.py:53
  525.6 3.5 collective-permute-done.50
  536.9 3.8 collective-permute-done.52
  (356 shorter events, 158.9 us)
Async XLA Ops:
  7.7 19.0 %collective-permute-start.12 = (bf16[1,3,48,384]{3,2,1,0:T(8,128)(2,1)S(1)}, bf16[1,3,48,384]{3,2,1,0:T(8,128)(2,1)S(1)}, u32[]{:S(2)}, u32[]{:S(2)}) collective-permute-start(bf16[1,3,48,384]{3,2,1,0:T(8,128)(2,1)S(1)} %get-tuple-element.142), channel_id=1, source_target_pairs={{0,8},{1,9},{2,10},{3,11},{4,12},{5,13},{6,14},{7,15},{8,0},{9,1},... | collective-permute-start | bytes 331784 | tf_op jit(solution)/shard_map/ppermute | solution.py:53
  8.5 20.9 %collective-permute-start.13 = (bf16[1,3,48,384]{3,2,1,0:T(8,128)(2,1)S(1)}, bf16[1,3,48,384]{3,2,1,0:T(8,128)(2,1)S(1)}, u32[]{:S(2)}, u32[]{:S(2)}) collective-permute-start(bf16[1,3,48,384]{3,2,1,0:T(8,128)(2,1)S(1)} %get-tuple-element.142), channel_id=1, source_target_pairs={{0,16},{1,17},{2,18},{3,19},{4,20},{5,21},{6,22},{7,23},{8,24},{9,... | collective-permute-start | bytes 331784 | tf_op jit(solution)/shard_map/ppermute | solution.py:53
  16.7 43.1 %collective-permute-start = (bf16[1,24,2432]{2,1,0:T(8,128)(2,1)S(1)}, bf16[1,24,2432]{2,1,0:T(8,128)(2,1)S(1)}, u32[]{:S(2)}, u32[]{:S(2)}) collective-permute-start(bf16[1,24,2432]{2,1,0:T(8,128)(2,1)S(1)} %fusion.17), channel_id=1, source_target_pairs={{0,8},{1,9},{2,10},{3,11},{4,12},{5,13},{6,14},{7,15},{8,0},{9,1},... | collective-permute-start | bytes 350216 | tf_op jit(solution)/shard_map/ppermute | solution.py:53
  17.1 43.1 %collective-permute-start.1 = (bf16[1,24,2432]{2,1,0:T(8,128)(2,1)S(1)}, bf16[1,24,2432]{2,1,0:T(8,128)(2,1)S(1)}, u32[]{:S(2)}, u32[]{:S(2)}) collective-permute-start(bf16[1,24,2432]{2,1,0:T(8,128)(2,1)S(1)} %fusion.17), channel_id=1, source_target_pairs={{0,16},{1,17},{2,18},{3,19},{4,20},{5,21},{6,22},{7,23},{8,24},{9,... | collective-permute-start | bytes 350216 | tf_op jit(solution)/shard_map/ppermute | solution.py:53
  26.6 35.8 %collective-permute-start.2 = (bf16[1,24,2432]{2,1,0:T(8,128)(2,1)S(1)}, bf16[1,24,2432]{2,1,0:T(8,128)(2,1)S(1)}, u32[]{:S(2)}, u32[]{:S(2)}) collective-permute-start(bf16[1,24,2432]{2,1,0:T(8,128)(2,1)S(1)} %fusion.17), channel_id=1, source_target_pairs={{0,24},{1,25},{2,26},{3,27},{4,28},{5,29},{6,30},{7,31},{8,16},{9,... | collective-permute-start | bytes 350216 | tf_op jit(solution)/shard_map/ppermute | solution.py:53
  62.4 50.2 %collective-permute-start.15 = (bf16[4,3,48,384]{3,2,1,0:T(8,128)(2,1)S(1)}, bf16[4,3,48,384]{3,2,1,0:T(8,128)(2,1)S(1)}, u32[]{:S(2)}, u32[]{:S(2)}) collective-permute-start(bf16[4,3,48,384]{3,2,1,0:T(8,128)(2,1)S(1)} %pad_maximum_fusion.7), channel_id=1, source_target_pairs={{0,4},{1,5},{2,6},{3,7},{4,0},{5,1},{6,2},{7,3},{8,12},{9,13},{10,... | collective-permute-start | bytes 1327112 | tf_op jit(solution)/shard_map/ppermute | solution.py:53
  64.0 50.3 %collective-permute-start.33 = (bf16[4,3,48,384]{3,2,1,0:T(8,128)(2,1)S(1)}, bf16[4,3,48,384]{3,2,1,0:T(8,128)(2,1)S(1)}, u32[]{:S(2)}, u32[]{:S(2)}) collective-permute-start(bf16[4,3,48,384]{3,2,1,0:T(8,128)(2,1)S(1)} %pad_maximum_fusion.10), channel_id=1, source_target_pairs={{0,1},{1,0},{2,3},{3,2},{4,5},{5,4},{6,7},{7,6},{8,9},{9,8},{10,11... | collective-permute-start | bytes 1327112 | tf_op jit(solution)/shard_map/ppermute | solution.py:53
  67.4 18.1 %collective-permute-start.3 = (bf16[4,24,2432]{2,1,0:T(8,128)(2,1)S(1)}, bf16[4,24,2432]{2,1,0:T(8,128)(2,1)S(1)}, u32[]{:S(2)}, u32[]{:S(2)}) collective-permute-start(bf16[4,24,2432]{2,1,0:T(8,128)(2,1)S(1)} %pad_maximum_fusion.5), channel_id=1, source_target_pairs={{0,4},{1,5},{2,6},{3,7},{4,0},{5,1},{6,2},{7,3},{8,12},{9,13},{10,... | collective-permute-start | bytes 1400840 | tf_op jit(solution)/shard_map/ppermute | solution.py:53
  69.0 22.7 %collective-permute-start.9 = (bf16[4,24,2816]{2,1,0:T(8,128)(2,1)S(1)}, bf16[4,24,2816]{2,1,0:T(8,128)(2,1)S(1)}, u32[]{:S(2)}, u32[]{:S(2)}) collective-permute-start(bf16[4,24,2816]{2,1,0:T(8,128)(2,1)S(1)} %pad_maximum_fusion.4), channel_id=1, source_target_pairs={{0,1},{1,0},{2,3},{3,2},{4,5},{5,4},{6,7},{7,6},{8,9},{9,8},{10,11... | collective-permute-start | bytes 1622024 | tf_op jit(solution)/shard_map/ppermute | solution.py:53
  73.5 43.2 %collective-permute-start.27 = (bf16[4,3,48,384]{3,2,1,0:T(8,128)(2,1)S(1)}, bf16[4,3,48,384]{3,2,1,0:T(8,128)(2,1)S(1)}, u32[]{:S(2)}, u32[]{:S(2)}) collective-permute-start(bf16[4,3,48,384]{3,2,1,0:T(8,128)(2,1)S(1)} %pad_maximum_fusion.9), channel_id=1, source_target_pairs={{0,4},{1,5},{2,6},{3,7},{4,0},{5,1},{6,2},{7,3},{8,12},{9,13},{10,... | collective-permute-start | bytes 1327112 | tf_op jit(solution)/shard_map/ppermute | solution.py:53
  85.5 53.7 %collective-permute-start.22 = (bf16[8,3,48,384]{3,2,1,0:T(8,128)(2,1)S(1)}, bf16[8,3,48,384]{3,2,1,0:T(8,128)(2,1)S(1)}, u32[]{:S(2)}, u32[]{:S(2)}) collective-permute-start(bf16[8,3,48,384]{3,2,1,0:T(8,128)(2,1)S(1)} %get-tuple-element.145), channel_id=1, source_target_pairs={{0,4},{1,5},{2,6},{3,7},{4,0},{5,1},{6,2},{7,3},{8,12},{9,13},{10,... | collective-permute-start | bytes 2654216 | tf_op jit(solution)/shard_map/ppermute | solution.py:53
  91.8 19.1 %collective-permute-start.4 = (bf16[8,24,2432]{2,1,0:T(8,128)(2,1)S(1)}, bf16[8,24,2432]{2,1,0:T(8,128)(2,1)S(1)}, u32[]{:S(2)}, u32[]{:S(2)}) collective-permute-start(bf16[8,24,2432]{2,1,0:T(8,128)(2,1)S(1)} %constant_dynamic-update-slice_fusion), channel_id=1, source_target_pairs={{0,1},{1,0},{2,3},{3,2},{4,5},{5,4},{6,7},{7,6},{8,9},{9,8},{10,11... | collective-permute-start | bytes 2801672 | tf_op jit(solution)/shard_map/ppermute | solution.py:53
  110.8 26.8 %collective-permute-start.10 = (bf16[4,48,2816]{2,1,0:T(8,128)(2,1)S(1)}, bf16[4,48,2816]{2,1,0:T(8,128)(2,1)S(1)}, u32[]{:S(2)}, u32[]{:S(2)}) collective-permute-start(bf16[4,48,2816]{2,1,0:T(8,128)(2,1)S(1)} %pad_maximum_fusion.2), channel_id=1, source_target_pairs={{0,4},{1,5},{2,6},{3,7},{4,0},{5,1},{6,2},{7,3},{8,12},{9,13},{10,... | collective-permute-start | bytes 3244040 | tf_op jit(solution)/shard_map/ppermute | solution.py:53
  112.6 43.7 %collective-permute-start.5 = (bf16[8,48,2432]{2,1,0:T(8,128)(2,1)S(1)}, bf16[8,48,2432]{2,1,0:T(8,128)(2,1)S(1)}, u32[]{:S(2)}, u32[]{:S(2)}) collective-permute-start(bf16[8,48,2432]{2,1,0:T(8,128)(2,1)S(1)} %pad_maximum_fusion.1.near), channel_id=1, source_target_pairs={{0,2},{1,3},{2,0},{3,1},{4,6},{5,7},{6,4},{7,5},{8,10},{9,11},{10,... | collective-permute-start | bytes 5603336 | tf_op jit(solution)/shard_map/ppermute | solution.py:53
  114.3 26.2 %collective-permute-start.16 = (bf16[8,3,48,384]{3,2,1,0:T(8,128)(2,1)S(1)}, bf16[8,3,48,384]{3,2,1,0:T(8,128)(2,1)S(1)}, u32[]{:S(2)}, u32[]{:S(2)}) collective-permute-start(bf16[8,3,48,384]{3,2,1,0:T(8,128)(2,1)S(1)} %get-tuple-element.147), channel_id=1, source_target_pairs={{0,1},{1,0},{2,3},{3,2},{4,5},{5,4},{6,7},{7,6},{8,9},{9,8},{10,11... | collective-permute-start | bytes 2654216 | tf_op jit(solution)/shard_map/ppermute | solution.py:53
  116.7 34.8 %collective-permute-start.34 = (bf16[8,3,48,384]{3,2,1,0:T(8,128)(2,1)S(1)}, bf16[8,3,48,384]{3,2,1,0:T(8,128)(2,1)S(1)}, u32[]{:S(2)}, u32[]{:S(2)}) collective-permute-start(bf16[8,3,48,384]{3,2,1,0:T(8,128)(2,1)S(1)} %get-tuple-element.129), channel_id=1, source_target_pairs={{0,4},{1,5},{2,6},{3,7},{4,0},{5,1},{6,2},{7,3},{8,12},{9,13},{10,... | collective-permute-start | bytes 2654216 | tf_op jit(solution)/shard_map/ppermute | solution.py:53
  139.2 41.5 %collective-permute-start.11 = (bf16[8,48,2816]{2,1,0:T(8,128)(2,1)S(1)}, bf16[8,48,2816]{2,1,0:T(8,128)(2,1)}, u32[]{:S(2)}, u32[]{:S(2)}) collective-permute-start(bf16[8,48,2816]{2,1,0:T(8,128)(2,1)S(1)} %pad_maximum_fusion.near), channel_id=1, source_target_pairs={{0,2},{1,3},{2,0},{3,1},{4,6},{5,7},{6,4},{7,5},{8,10},{9,11},{10,... | collective-permute-start | bytes 6488072 | tf_op jit(solution)/shard_map/ppermute | solution.py:53
  140.5 60.0 %collective-permute-start.23 = (bf16[16,3,48,384]{3,2,1,0:T(8,128)(2,1)}, bf16[16,3,48,384]{3,2,1,0:T(8,128)(2,1)}, u32[]{:S(2)}, u32[]{:S(2)}) collective-permute-start(bf16[16,3,48,384]{3,2,1,0:T(8,128)(2,1)} %constant_dynamic-update-slice_fusion.21.refs_2_), channel_id=1, source_target_pairs={{0,2},{1,3},{2,0},{3,1},{4,6},{5,7},{6,4},{7,5},{8,10},{9,11},{10,... | collective-permute-start | bytes 5308424 | tf_op jit(solution)/shard_map/ppermute | solution.py:53
  151.5 49.1 %collective-permute-start.17 = (bf16[16,3,48,384]{3,2,1,0:T(8,128)(2,1)}, bf16[16,3,48,384]{3,2,1,0:T(8,128)(2,1)}, u32[]{:S(2)}, u32[]{:S(2)}) collective-permute-start(bf16[16,3,48,384]{3,2,1,0:T(8,128)(2,1)} %constant_dynamic-update-slice_fusion.10.refs_0_), channel_id=1, source_target_pairs={{0,2},{1,3},{2,0},{3,1},{4,6},{5,7},{6,4},{7,5},{8,10},{9,11},{10,... | collective-permute-start | bytes 5308424 | tf_op jit(solution)/shard_map/ppermute | solution.py:53
  155.2 80.4 %collective-permute-start.35 = (bf16[16,3,48,384]{3,2,1,0:T(8,128)(2,1)}, bf16[16,3,48,384]{3,2,1,0:T(8,128)(2,1)}, u32[]{:S(2)}, u32[]{:S(2)}) collective-permute-start(bf16[16,3,48,384]{3,2,1,0:T(8,128)(2,1)} %constant_dynamic-update-slice_fusion.43.refs_4_), channel_id=1, source_target_pairs={{0,2},{1,3},{2,0},{3,1},{4,6},{5,7},{6,4},{7,5},{8,10},{9,11},{10,... | collective-permute-start | bytes 5308424 | tf_op jit(solution)/shard_map/ppermute | solution.py:53
  156.3 79.4 %collective-permute-start.29 = (bf16[16,3,48,384]{3,2,1,0:T(8,128)(2,1)}, bf16[16,3,48,384]{3,2,1,0:T(8,128)(2,1)}, u32[]{:S(2)}, u32[]{:S(2)}) collective-permute-start(bf16[16,3,48,384]{3,2,1,0:T(8,128)(2,1)} %constant_dynamic-update-slice_fusion.32.refs_2_), channel_id=1, source_target_pairs={{0,2},{1,3},{2,0},{3,1},{4,6},{5,7},{6,4},{7,5},{8,10},{9,11},{10,... | collective-permute-start | bytes 5308424 | tf_op jit(solution)/shard_map/ppermute | solution.py:53
  359.7 44.7 %collective-permute-start.60 = (bf16[16,3,48,384]{3,2,1,0:T(8,128)(2,1)}, bf16[16,3,48,384]{3,2,1,0:T(8,128)(2,1)}, u32[]{:S(2)}, u32[]{:S(2)}) collective-permute-start(bf16[16,3,48,384]{3,2,1,0:T(8,128)(2,1)} %get-tuple-element.86), channel_id=1, source_target_pairs={{0,2},{1,3},{2,0},{3,1},{4,6},{5,7},{6,4},{7,5},{8,10},{9,11},{10,... | collective-permute-start | bytes 5308424 | tf_op jit(solution)/shard_map/ppermute | solution.py:53
  360.2 46.7 %collective-permute-start.66 = (bf16[16,3,48,384]{3,2,1,0:T(8,128)(2,1)}, bf16[16,3,48,384]{3,2,1,0:T(8,128)(2,1)S(1)}, u32[]{:S(2)}, u32[]{:S(2)}) collective-permute-start(bf16[16,3,48,384]{3,2,1,0:T(8,128)(2,1)} %get-tuple-element.88), channel_id=1, source_target_pairs={{0,2},{1,3},{2,0},{3,1},{4,6},{5,7},{6,4},{7,5},{8,10},{9,11},{10,... | collective-permute-start | bytes 5308424 | tf_op jit(solution)/shard_map/ppermute | solution.py:53
  406.3 22.5 %collective-permute-start.61 = (bf16[8,3,48,384]{3,2,1,0:T(8,128)(2,1)S(1)}, bf16[8,3,48,384]{3,2,1,0:T(8,128)(2,1)S(1)}, u32[]{:S(2)}, u32[]{:S(2)}) collective-permute-start(bf16[8,3,48,384]{3,2,1,0:T(8,128)(2,1)S(1)} %slice.690), channel_id=1, source_target_pairs={{0,4},{1,5},{2,6},{3,7},{4,0},{5,1},{6,2},{7,3},{8,12},{9,13},{10,... | collective-permute-start | bytes 2654216 | tf_op jit(solution)/shard_map/ppermute | solution.py:53
  408.1 22.5 %collective-permute-start.67 = (bf16[8,3,48,384]{3,2,1,0:T(8,128)(2,1)S(1)}, bf16[8,3,48,384]{3,2,1,0:T(8,128)(2,1)S(1)}, u32[]{:S(2)}, u32[]{:S(2)}) collective-permute-start(bf16[8,3,48,384]{3,2,1,0:T(8,128)(2,1)S(1)} %slice.689), channel_id=1, source_target_pairs={{0,1},{1,0},{2,3},{3,2},{4,5},{5,4},{6,7},{7,6},{8,9},{9,8},{10,11... | collective-permute-start | bytes 2654216 | tf_op jit(solution)/shard_map/ppermute | solution.py:53
  410.3 37.5 %collective-permute-start.73 = (bf16[8,3,48,384]{3,2,1,0:T(8,128)(2,1)S(1)}, bf16[8,3,48,384]{3,2,1,0:T(8,128)(2,1)S(1)}, u32[]{:S(2)}, u32[]{:S(2)}) collective-permute-start(bf16[8,3,48,384]{3,2,1,0:T(8,128)(2,1)S(1)} %slice.688), channel_id=1, source_target_pairs={{0,4},{1,5},{2,6},{3,7},{4,0},{5,1},{6,2},{7,3},{8,12},{9,13},{10,... | collective-permute-start | bytes 2654216 | tf_op jit(solution)/shard_map/ppermute | solution.py:53
  412.1 37.5 %collective-permute-start.79 = (bf16[8,3,48,384]{3,2,1,0:T(8,128)(2,1)S(1)}, bf16[8,3,48,384]{3,2,1,0:T(8,128)(2,1)S(1)}, u32[]{:S(2)}, u32[]{:S(2)}) collective-permute-start(bf16[8,3,48,384]{3,2,1,0:T(8,128)(2,1)S(1)} %slice.687), channel_id=1, source_target_pairs={{0,1},{1,0},{2,3},{3,2},{4,5},{5,4},{6,7},{7,6},{8,9},{9,8},{10,11... | collective-permute-start | bytes 2654216 | tf_op jit(solution)/shard_map/ppermute | solution.py:53
  414.0 100.2 %collective-permute-start.49 = (bf16[8,24,2816]{2,1,0:T(8,128)(2,1)S(1)}, bf16[8,24,2816]{2,1,0:T(8,128)(2,1)S(1)}, u32[]{:S(2)}, u32[]{:S(2)}) collective-permute-start(bf16[8,24,2816]{2,1,0:T(8,128)(2,1)S(1)} %dynamic-slice_convert_fusion), channel_id=1, source_target_pairs={{0,1},{1,0},{2,3},{3,2},{4,5},{5,4},{6,7},{7,6},{8,9},{9,8},{10,11... | collective-permute-start | bytes 3244040 | tf_op jit(solution)/shard_map/ppermute | solution.py:53
  429.0 53.2 %collective-permute-start.62 = (bf16[4,3,48,384]{3,2,1,0:T(8,128)(2,1)S(1)}, bf16[4,3,48,384]{3,2,1,0:T(8,128)(2,1)S(1)}, u32[]{:S(2)}, u32[]{:S(2)}) collective-permute-start(bf16[4,3,48,384]{3,2,1,0:T(8,128)(2,1)S(1)} %slice.695), channel_id=1, source_target_pairs={{0,1},{1,0},{2,3},{3,2},{4,5},{5,4},{6,7},{7,6},{8,9},{9,8},{10,11... | collective-permute-start | bytes 1327112 | tf_op jit(solution)/shard_map/ppermute | solution.py:53
  430.9 52.5 %collective-permute-start.68 = (bf16[4,3,48,384]{3,2,1,0:T(8,128)(2,1)S(1)}, bf16[4,3,48,384]{3,2,1,0:T(8,128)(2,1)S(1)}, u32[]{:S(2)}, u32[]{:S(2)}) collective-permute-start(bf16[4,3,48,384]{3,2,1,0:T(8,128)(2,1)S(1)} %slice.694), channel_id=1, source_target_pairs={{0,4},{1,5},{2,6},{3,7},{4,0},{5,1},{6,2},{7,3},{8,12},{9,13},{10,... | collective-permute-start | bytes 1327112 | tf_op jit(solution)/shard_map/ppermute | solution.py:53
  448.0 43.4 %collective-permute-start.74 = (bf16[4,3,48,384]{3,2,1,0:T(8,128)(2,1)S(1)}, bf16[4,3,48,384]{3,2,1,0:T(8,128)(2,1)S(1)}, u32[]{:S(2)}, u32[]{:S(2)}) collective-permute-start(bf16[4,3,48,384]{3,2,1,0:T(8,128)(2,1)S(1)} %slice.693), channel_id=1, source_target_pairs={{0,1},{1,0},{2,3},{3,2},{4,5},{5,4},{6,7},{7,6},{8,9},{9,8},{10,11... | collective-permute-start | bytes 1327112 | tf_op jit(solution)/shard_map/ppermute | solution.py:53
  449.8 44.1 %collective-permute-start.80 = (bf16[4,3,48,384]{3,2,1,0:T(8,128)(2,1)S(1)}, bf16[4,3,48,384]{3,2,1,0:T(8,128)(2,1)S(1)}, u32[]{:S(2)}, u32[]{:S(2)}) collective-permute-start(bf16[4,3,48,384]{3,2,1,0:T(8,128)(2,1)S(1)} %slice.692), channel_id=1, source_target_pairs={{0,4},{1,5},{2,6},{3,7},{4,0},{5,1},{6,2},{7,3},{8,12},{9,13},{10,... | collective-permute-start | bytes 1327112 | tf_op jit(solution)/shard_map/ppermute | solution.py:53
  (79 other events, 765.8 us)
